TPU v7x, 32 devices: a whole 2x2x4 slice. The times are simulated.
32 devices in a mesh: pheno: 2 (over x), samp: 8 (over z, y), var: 2 (over core).
Axes of the slice: x: 2, y: 2, z: 4, core: 2. Of those that a mesh axis runs over, the one named last changes fastest.
Arguments:
- genotypes: bfloat16 [4608, 16384], P('samp', 'var'), may hold values from -6 to 6, as said below
- coefficients: float32 [64, 16384], P('pheno', 'var'), parts along dimension 0, may hold values from -0.5 to 0.5
- time_order: int32 [9216], P(('pheno', 'samp')), parts along dimension 0, may hold values from 0 to 4607, as said below
- fold_label: int32 [9216], P(('pheno', 'samp')), parts along dimension 0, may hold values from 0 to 7
- event_flag: int32 [9216], P(('pheno', 'samp')), parts along dimension 0, may hold values 0 or 1
- penalty: float32 [32], replicated, may hold values from 0.3 to 1.5
- step_size: float32 [32], replicated, may hold values from 0.2 to 1
Outputs:
- coefficients_out: float32 [64, 16384], P('pheno', 'var'), parts along dimension 0
- score: bfloat16 [64, 4608], P('pheno', 'samp'), parts along dimension 0
There are 2 independent parts, one for each index of `pheno`. A program takes and returns all parts, laid end to end along the dimension named above; an argument that names none is the same for every part. Nothing has to cross between parts.
Inputs may be any that keep to these rules, and one draw needn't show every extreme that they name: time_order names every sample ID once; each block of 576 consecutive IDs holds exactly 576 / 8 of the IDs in each block of 576 consecutive time ranks. `genotypes`: entries of mean zero and unit variance.
All inputs are finite; a program needn't handle non-finite values. No bound on the sum of `event_flag` on one device may be relied on, other than what follows from the above.
Results may differ from a plain program's by a relative error of at most 0.0027.
Values may be sent and summed in bfloat16 or wider, within the bound.
A program may use at most 64 MiB of HBM per device.

v0:
```python
import functools
import math

import jax
import jax.numpy as jnp
from jax import lax
from jax.experimental import pallas as pl
from jax.experimental.pallas import tpu as pltpu
from jax.sharding import PartitionSpec as P

VARS = 16384
FOLDS = 8
ITERS = 3
MESH = pl.DeviceIdType.MESH
CUTS_LOW = 1
CUTS = 4
F32 = jnp.float32
BF16 = jnp.bfloat16


def each(count, body):
    if count <= 8:
        for step in range(count):
            body(step)
    else:
        lax.fori_loop(0, count, lambda step, carry: (body(step), carry)[1], 0)


def halves(value):
    high = value.astype(BF16)
    low = (value - high.astype(F32)).astype(BF16)
    return jnp.concatenate([high, low], axis=0)


def across(left, right):
    return lax.dot_general(left, right, (((1,), (1,)), ((), ())), preferred_element_type=F32)


def across2(value, matrix):
    rows = value.shape[0]
    both = across(halves(value), matrix)
    return both[:rows] + both[rows:]


def dot2(value, matrix):
    rows = value.shape[0]
    both = jnp.dot(halves(value), matrix, preferred_element_type=F32)
    return both[:rows] + both[rows:]


def path_kernel(
    count, scale_vars, scale_samples,
    geno_in, coef_in, code_row, place_out, reach, back, spot, step_row, penalty_row,
    coef_out, score_out,
    geno, to_time, later, earlier, to_id, mask, kept, kept_time, place_in, code_out, code_in,
    low, shard, half_send, half_recv, out_a, in_a, out_b, in_b, out_g, in_g, pred, held, s_ss, s_rs,
    load_sem, p_ss, p_rs, l_ss, l_rs, fwd_ss, last_ss, half_ss, half_rs, a_ss, a_rs, b_ss, b_rs, g_ss, g_rs, c_ss, c_rs, f_ss, f_rs,
):
    me = lax.axis_index("samp")
    var = lax.axis_index("var")
    columns, variants = coef_in.shape
    rows = geno.shape[0]
    part = variants // count
    width = later.shape[1] // count
    share = rows // count
    half = count // 2
    few = columns // 2
    mine = pl.ds(pl.multiple_of(var * few, few), few)
    theirs = pl.ds(pl.multiple_of((1 - var) * few, few), few)
    load = pltpu.make_async_copy(geno_in, geno, load_sem)
    load.start()

    def peer(step):
        return lax.rem(me + step, count)

    def piece(owner):
        return pl.ds(pl.multiple_of(owner * part, part), part)

    side = 1 - 2 * lax.rem(me, 2)

    def down(step):
        return lax.rem(me + 2 * step, count)

    cut = columns // CUTS
    cut_low = columns // CUTS_LOW

    def bit(owner, number):
        return low.at[owner, pl.ds(number * cut_low, cut_low), :]

    def wide(owner, number):
        return coef_out.at[pl.ds(number * cut, cut), piece(owner)]

    def send_to(spot_of, ssem, rsem, number, owner):
        return pltpu.make_async_remote_copy(
            src_ref=spot_of(me, number), dst_ref=spot_of(me, number),
            send_sem=ssem.at[owner, number], recv_sem=rsem.at[me, number],
            device_id={"samp": owner}, device_id_type=MESH,
        )

    def pass_on(spot_of, ssem, rsem, number, owner):
        return pltpu.make_async_remote_copy(
            src_ref=spot_of(owner, number), dst_ref=spot_of(owner, number),
            send_sem=ssem.at[owner, number], recv_sem=rsem.at[owner, number],
            device_id={"samp": me + side}, device_id_type=MESH,
        )

    def spread_out(spot_of, ssem, rsem):
        for number in range(CUTS_LOW if spot_of is bit else CUTS):
            def go(step):
                send_to(spot_of, ssem, rsem, number, down(step + 1)).start()
            send_to(spot_of, ssem, rsem, number, me + side).start()
            each(half - 1, go)

    def relay_all(spot_of, ssem, rsem):
        for number in range(CUTS_LOW if spot_of is bit else CUTS):
            def go(step):
                copy = pass_on(spot_of, ssem, rsem, number, down(step + 1))
                copy.wait_recv()
                copy.start()
            each(half - 1, go)

    def land(spot_of, ssem, rsem, owner):
        for number in range(CUTS_LOW if spot_of is bit else CUTS):
            pass_on(spot_of, ssem, rsem, number, owner).wait_recv()

    def settle(spot_of, ssem, fsem, rsem):
        for number in range(CUTS_LOW if spot_of is bit else CUTS):
            def go(step):
                owner = down(step + 1)
                send_to(spot_of, ssem, rsem, number, owner).wait_send()
                pass_on(spot_of, fsem, rsem, number, owner).wait_send()
            each(half - 1, go)
            send_to(spot_of, ssem, rsem, number, me + side).wait_send()

    def slots(owner):
        return pl.ds(pl.multiple_of(owner * width, width), width)

    barrier = pltpu.get_barrier_semaphore()

    def greet(step):
        pl.semaphore_signal(barrier, inc=1, device_id={"samp": peer(step + 1)}, device_id_type=MESH)

    each(count - 1, greet)
    pl.semaphore_signal(barrier, inc=1, device_id={"var": 1 - var}, device_id_type=MESH)
    pl.semaphore_wait(barrier, count)

    def send(source, target, ssem, rsem, owner):
        return pltpu.make_async_remote_copy(
            src_ref=source,
            dst_ref=target,
            send_sem=ssem.at[owner],
            recv_sem=rsem.at[me],
            device_id={"samp": owner},
            device_id_type=MESH,
        )

    def arrive(source, target, ssem, rsem, owner):
        pltpu.make_async_remote_copy(
            src_ref=source,
            dst_ref=target,
            send_sem=ssem.at[owner],
            recv_sem=rsem.at[owner],
            device_id={"samp": owner},
            device_id_type=MESH,
        ).wait_recv()

    def push_p(step):
        owner = peer(step + 1)
        send(place_out.at[owner], place_in.at[me], p_ss, p_rs, owner).start()
    each(count - 1, push_p)

    line = lax.broadcasted_iota(jnp.int32, (8, rows), 0)
    labels = jnp.where(line == 0, code_row[...] // 2, jnp.where(line == 1, code_row[...] % 2, 0)).astype(F32)
    same = lax.broadcasted_iota(jnp.int32, (columns, columns), 0) == lax.broadcasted_iota(
        jnp.int32, (columns, columns), 1
    )
    pace = jnp.sum(jnp.where(same, step_row[...], 0.0), axis=1, keepdims=True)
    threshold = pace * jnp.sum(jnp.where(same, penalty_row[...], 0.0), axis=1, keepdims=True)
    column_fold = lax.rem(lax.broadcasted_iota(jnp.int32, (few, rows), 0) + var * few, FOLDS).astype(F32)
    mask[...] = jnp.where(labels[0:1, :] != column_fold, 1.0, 0.0)
    kept[...] = mask[...] * labels[1:2, :]
    ranks = lax.broadcasted_iota(jnp.int32, (rows, width), 0)
    lane = lax.broadcasted_iota(jnp.int32, (rows, width), 1)
    for owner in range(count):
        span = slice(owner * width, (owner + 1) * width)
        later[:, span] = jnp.where(reach[owner] >= ranks, 1.0, 0.0).astype(BF16)
        earlier[:, span] = jnp.where(back[owner] >= ranks, 1.0, 0.0).astype(BF16)

    place_in[me] = place_out[me]
    block = jnp.zeros((rows, width), jnp.int32)
    def land_p(step):
        owner = peer(step + 1)
        arrive(place_out.at[owner], place_in.at[owner], p_ss, p_rs, owner)
        send(place_out.at[owner], place_in.at[me], p_ss, p_rs, owner).wait_send()
    each(count - 1, land_p)
    for owner in range(1, count):
        block += jnp.where(place_in[owner] == ranks, owner, 0)
    block = jnp.broadcast_to(jnp.sum(block, axis=1, keepdims=True), (rows, width))
    in_totals = (lane - share) == block
    for owner in range(count):
        span = slice(owner * width, (owner + 1) * width)
        hit = place_in[owner] == ranks
        to_time[:, span] = jnp.where(hit | in_totals, 1.0, 0.0).astype(BF16)
        to_id[:, span] = jnp.where(hit | ((lane == share) & (block > owner)), 1.0, 0.0).astype(BF16)
    spread = jnp.dot(labels.astype(BF16), to_time[...], preferred_element_type=F32)
    for owner in range(count):
        code_out[owner] = spread[:, owner * width:(owner + 1) * width]

    def push_l(step):
        owner = peer(step + 1)
        send(code_out.at[owner], code_in.at[me], l_ss, l_rs, owner).start()
    each(count - 1, push_l)
    code_in[me] = code_out[me]

    def land_l(step):
        owner = peer(step + 1)
        arrive(code_out.at[owner], code_in.at[owner], l_ss, l_rs, owner)
        send(code_out.at[owner], code_in.at[me], l_ss, l_rs, owner).wait_send()
    each(count - 1, land_l)
    labels_time = jnp.zeros((labels.shape[0], rows), F32)
    for owner in range(count):
        labels_time += across(
            code_in[owner].astype(BF16), jnp.where(spot[owner] == ranks, 1.0, 0.0).astype(BF16)
        )
    kept_time[...] = jnp.where(labels_time[0:1, :] != column_fold, 1.0, 0.0) * labels_time[1:2, :]

    def fill(step):
        low[step] = coef_in[:, piece(step)].astype(BF16)

    each(count, fill)
    shard[...] = coef_in[:, piece(me)]
    load.wait()

    def one_step(turn, carry):
        pred[...] = jnp.zeros_like(pred)

        def add_part(owner):
            pred[...] += across(low[owner], geno[:, piece(owner)])

        def add_down(step):
            add_part(down(step + 1))

        def add_side(step):
            owner = down(step) + side

            @pl.when(turn > 0)
            def _():
                land(bit, c_ss, c_rs, owner)
            add_part(owner)

        add_part(me)

        @pl.when(turn > 0)
        def _():
            relay_all(bit, fwd_ss, c_rs)
        each(half - 1, add_down)
        each(half, add_side)
        half_send[...] = pred[theirs, :]
        slot = lax.rem(turn, 2)
        swap = pltpu.make_async_remote_copy(
            src_ref=half_send, dst_ref=half_recv.at[slot], send_sem=half_ss, recv_sem=half_rs.at[slot],
            device_id={"var": 1 - var}, device_id_type=MESH,
        )
        swap.start()
        swap.wait()

        @pl.when(turn > 0)
        def _():
            settle(bit, c_ss, fwd_ss, c_rs)

        weight = mask[...] * jnp.exp((pred[mine, :] + half_recv[slot]) * scale_vars)
        held[...] = weight
        spread = dot2(weight, to_time[...])
        for owner in range(count):
            out_a[owner] = spread[:, owner * width:(owner + 1) * width]

        def push_a(step):
            owner = peer(step + 1)
            send(out_a.at[owner], in_a.at[me], a_ss, a_rs, owner).start()
        each(count - 1, push_a)
        risk = across2(out_a[me], later[:, slots(me)])
        for step in range(count - 1):
            owner = peer(step + 1)
            arrive(out_a.at[owner], in_a.at[owner], a_ss, a_rs, owner)
            risk += across2(in_a[owner], later[:, slots(owner)])
        events = kept_time[...]
        ratio = events / jnp.where(events > 0, risk, 1.0)
        spread = dot2(ratio, earlier[...])
        for owner in range(count):
            out_b[owner] = spread[:, owner * width:(owner + 1) * width]

        def push_b(step):
            owner = peer(step + 1)
            send(out_b.at[owner], in_b.at[me], b_ss, b_rs, owner).start()
        each(count - 1, push_b)
        hazard = across2(out_b[me], to_id[:, slots(me)])
        for step in range(count - 1):
            owner = peer(step + 1)
            arrive(out_b.at[owner], in_b.at[owner], b_ss, b_rs, owner)
            hazard += across2(in_b[owner], to_id[:, slots(owner)])
        score_out[mine, :] = (held[...] * hazard - kept[...]).astype(BF16)
        trade = pltpu.make_async_remote_copy(
            src_ref=score_out.at[mine, :], dst_ref=score_out.at[mine, :], send_sem=s_ss, recv_sem=s_rs,
            device_id={"var": 1 - var}, device_id_type=MESH,
        )
        trade.start()
        trade.wait()

        def push_g(step):
            owner = peer(step + 1)
            out_g[owner] = jnp.dot(
                score_out[...], geno[:, piece(owner)], preferred_element_type=F32
            ).astype(out_g.dtype)
            send(out_g.at[owner], in_g.at[me], g_ss, g_rs, owner).start()
        each(count - 1, push_g)
        total = jnp.dot(score_out[...], geno[:, piece(me)], preferred_element_type=F32)
        for step in range(count - 1):
            owner = peer(count - 1 - step)
            arrive(out_g.at[owner], in_g.at[owner], g_ss, g_rs, owner)
            total += in_g[owner].astype(F32)
        stepped = shard[...] - pace * (total * scale_samples)
        shrunk = jnp.maximum(jnp.abs(stepped) - threshold, 0.0)
        fresh = jnp.where(stepped > 0, shrunk, -shrunk)
        shard[...] = fresh

        def drained_all(step):
            owner = peer(step + 1)
            send(out_a.at[owner], in_a.at[me], a_ss, a_rs, owner).wait_send()
            send(out_b.at[owner], in_b.at[me], b_ss, b_rs, owner).wait_send()
            send(out_g.at[owner], in_g.at[me], g_ss, g_rs, owner).wait_send()

        @pl.when(turn < ITERS - 1)
        def _():
            low[me] = fresh.astype(BF16)

            spread_out(bit, c_ss, c_rs)

        each(count - 1, drained_all)
        return carry

    lax.fori_loop(0, ITERS, one_step, 0)

    coef_out[:, piece(me)] = shard[...]

    spread_out(wide, f_ss, f_rs)
    relay_all(wide, last_ss, f_rs)

    def land_f(step):
        land(wide, f_ss, f_rs, down(step) + side)
    each(half, land_f)
    settle(wide, f_ss, last_ss, f_rs)


def local(genotypes, coefficients, time_order, fold_label, event_flag, penalty, step_size):
    rows = genotypes.shape[0]
    columns, variants = coefficients.shape
    count = lax.axis_size("samp")
    me = lax.axis_index("samp")
    share = rows // count
    width = -(-(share + count) // 128) * 128
    total = count * width
    part = variants // count

    ranks = jnp.arange(rows, dtype=jnp.int32)
    slot_all = jnp.arange(total, dtype=jnp.int32)
    lane = slot_all % width
    owner = time_order // rows
    place = time_order % rows
    same = (owner[:, None] == owner[None, :]) & (ranks[:, None] < ranks[None, :])
    key = owner * width + jnp.sum(same.astype(jnp.int32), axis=0)
    match = key[:, None] == slot_all[None, :]
    rank_of = jnp.max(jnp.where(match, ranks[:, None], -1), axis=0)
    place_of = jnp.max(jnp.where(match, place[:, None], -1), axis=0)
    in_totals = (lane >= share) & (lane < share + count)
    spot = jnp.where(lane < share, rank_of, -1)
    reach = jnp.where(in_totals & (lane - share > me), rows, spot)
    back = jnp.where(lane == share, rows, spot)
    place_of, reach, back, spot = (value.reshape(count, 1, width) for value in (place_of, reach, back, spot))

    vmem = pl.BlockSpec(memory_space=pltpu.VMEM)
    dma = pltpu.SemaphoreType.DMA
    return pl.pallas_call(
        functools.partial(path_kernel, count, 1.0 / math.sqrt(VARS), 1.0 / math.sqrt(rows * count)),
        out_shape=(
            jax.ShapeDtypeStruct((columns, variants), F32),
            jax.ShapeDtypeStruct((columns, rows), BF16),
        ),
        in_specs=[pl.BlockSpec(memory_space=pl.ANY)] + [vmem] * 8,
        out_specs=(vmem, vmem),
        scratch_shapes=[
            pltpu.VMEM((rows, variants), BF16),
            pltpu.VMEM((rows, total), BF16),
            pltpu.VMEM((rows, total), BF16),
            pltpu.VMEM((rows, total), BF16),
            pltpu.VMEM((rows, total), BF16),
            pltpu.VMEM((columns // 2, rows), F32),
            pltpu.VMEM((columns // 2, rows), F32),
            pltpu.VMEM((columns // 2, rows), F32),
            pltpu.VMEM((count, 1, width), jnp.int32),
            pltpu.VMEM((count, 8, width), F32),
            pltpu.VMEM((count, 8, width), F32),
            pltpu.VMEM((count, columns, part), BF16),
            pltpu.VMEM((columns, part), F32),
            pltpu.VMEM((columns // 2, rows), F32),
            pltpu.VMEM((2, columns // 2, rows), F32),
            pltpu.VMEM((count, columns // 2, width), F32),
            pltpu.VMEM((count, columns // 2, width), F32),
            pltpu.VMEM((count, columns // 2, width), F32),
            pltpu.VMEM((count, columns // 2, width), F32),
            pltpu.VMEM((count, columns, part), BF16),
            pltpu.VMEM((count, columns, part), BF16),
            pltpu.VMEM((columns, rows), F32),
            pltpu.VMEM((columns // 2, rows), F32),
            dma, dma,
            dma,
        ] + [dma((count,))] * 4 + [dma((count, CUTS))] * 2 + [
            dma, dma((2,)),
        ] + [dma((count,))] * 6 + [dma((count, CUTS))] * 4,
        compiler_params=pltpu.CompilerParams(
            collective_id=0, has_side_effects=True, vmem_limit_bytes=60 * 1024 * 1024
        ),
    )(
        genotypes, coefficients, (fold_label * 2 + event_flag)[None], place_of, reach, back, spot,
        step_size[None], penalty[None],
    )


def solution(mesh):
    placed = (
        P("samp", "var"),
        P("pheno", "var"),
        P(("pheno", "samp")),
        P(("pheno", "samp")),
        P(("pheno", "samp")),
        P(),
        P(),
    )
    return jax.shard_map(
        local,
        mesh=mesh,
        in_specs=placed,
        out_specs=(P("pheno", "var"), P("pheno", "samp")),
        check_vma=False,
    )
```

profile of v0, /device:TPU:0, one launch (start us, length us, event | category | flops | bytes accessed | tf_op | source)
XLA Modules:
  0.0 152.4 jit_solution(2113255937619801436)
XLA Ops:
  0.6 0.7 multiply_add_fusion.1
  1.3 0.6 broadcast_in_dim.44.code_row
  1.9 0.7 add_select_fusion.1
  2.6 0.2 convert_reduce_fusion
  2.9 0.7 add_select_fusion
  3.6 1.3 select_reduce_fusion
  4.9 0.6 compare_select_fusion.2
  5.5 0.0 copy-start
  5.5 0.6 and_select_fusion.reach
  6.1 0.0 copy-done
  6.1 142.7 %shard_map.86 = (f32[32,8192]{1,0:T(8,128)}, bf16[32,576]{1,0:T(8,128)(2,1)}) custom-call(bf16[576,8192]{1,0:T(8,128)(2,1)} %geno_in.1, f32[32,8192]{1,0:T(8,128)} %coef_in.1, s32[1,576]{1,0:T(1,128)} %broadcast_in_dim.44.code_row, s32[8,1,128]{2,1,0:T(1,128)} %bitcast.4, s32[8,1,128]{2,1,0:T(1,128)} %and_select_fusion.reach, ...), custom_call_target="tpu_custom_call" | custom-call | tf_op jit(solution)/shard_map/pallas_call | solution.py:382
  148.8 2.3 %copy.11 = f32[32,8192]{1,0:T(8,128)} copy(f32[32,8192]{1,0:T(8,128)} %get-tuple-element.10) | data formatting | bytes 2097152
  151.1 1.4 copy.12
Async XLA Ops:
  5.5 0.6 copy-start
where the time goes:
time: 153 us; the launch traced here: 152 us
  Pallas kernels  143 us (93%)
  other arithmetic  4.82 us (3%)
  local copies, waits for them, and re-layouts  4.26 us (3%)
    pallas_call x1, Pallas kernels, local(): pl.pallas_call(functools.partial(path_kernel, count, 1.0 / math.sqrt(VARS...  143 us
    unnamed x4, local copies, waits for them, and re-layouts  3.67 us

commit v1 on v0

v1 whole, which is shorter than its diff:
```python
import functools
import math

import jax
import jax.numpy as jnp
from jax import lax
from jax.experimental import pallas as pl
from jax.experimental.pallas import tpu as pltpu
from jax.sharding import PartitionSpec as P

VARS = 16384
FOLDS = 8
ITERS = 3
MESH = pl.DeviceIdType.MESH
CUTS_LOW = 1
CUTS_SUM = 2
CUTS_LAST = 2
F32 = jnp.float32
BF16 = jnp.bfloat16


def each(count, body):
    if count <= 8:
        for step in range(count):
            body(step)
    else:
        lax.fori_loop(0, count, lambda step, carry: (body(step), carry)[1], 0)


def halves(value):
    high = value.astype(BF16)
    low = (value - high.astype(F32)).astype(BF16)
    return jnp.concatenate([high, low], axis=0)


def across(left, right):
    return lax.dot_general(left, right, (((1,), (1,)), ((), ())), preferred_element_type=F32)


def across2(value, matrix):
    rows = value.shape[0]
    both = across(halves(value), matrix)
    return both[:rows] + both[rows:]


def dot2(value, matrix):
    rows = value.shape[0]
    both = jnp.dot(halves(value), matrix, preferred_element_type=F32)
    return both[:rows] + both[rows:]


def path_kernel(
    count, scale_vars, scale_samples,
    geno_in, coef_in, codes, step_row, penalty_row,
    low_out, change_out, score_out,
    geno, coef, to_time, later, earlier, to_id, mask, kept, kept_time, place_out, place_in, spot, code_out, code_in,
    low, change, shard, half_send, half_recv, out_a, in_a, out_b, in_b,
    out_y, in_y, out_z, in_z, own_g, pred, held, score, score_wide,
    geno_sem, coef_sem, end_sem, change_sem, s_ss, s_rs, half_ss, half_rs, p_ss, p_rs, l_ss, l_rs, a_ss, a_rs, b_ss, b_rs,
    y_ss, y_rs, z_ss, z_rs, c_ss, c_rs, fwd_ss, fwd_rs, f_ss, f_rs, last_ss, last_rs,
):
    me = lax.axis_index("samp")
    var = lax.axis_index("var")
    columns, variants = coef.shape
    rows = geno.shape[0]
    part = variants // count
    width = later.shape[1] // count
    share = rows // count
    half = count // 2
    few = columns // 2
    mine = pl.ds(pl.multiple_of(var * few, few), few)
    theirs = pl.ds(pl.multiple_of((1 - var) * few, few), few)
    side = 1 - 2 * lax.rem(me, 2)

    def peer(step):
        return lax.rem(me + step, count)

    def down(hop):
        return lax.rem(me + 2 * hop, count)

    def up(hop):
        return lax.rem(me + count - 2 * hop, count)

    def piece(owner):
        return pl.ds(pl.multiple_of(owner * part, part), part)

    def band(number, cuts):
        cut = columns // cuts
        return pl.ds(number * cut, cut)

    def hops(body):
        if half <= 8:
            for hop in sorted(range(1, half), key=lambda hop: (abs(2 * hop - half), hop)):
                body(hop)
        else:
            lax.fori_loop(1, half, lambda hop, carry: (body(hop), carry)[1], 0)

    def slots(owner):
        return pl.ds(pl.multiple_of(owner * width, width), width)

    def block_load(owner):
        return pltpu.make_async_copy(geno_in.at[:, piece(owner)], geno.at[:, piece(owner)], geno_sem.at[owner])

    coef_load = pltpu.make_async_copy(coef_in, coef, coef_sem)
    coef_load.start()
    each(count, lambda owner: block_load(owner).start())

    barrier = pltpu.get_barrier_semaphore()

    def greet(step):
        pl.semaphore_signal(barrier, inc=1, device_id={"samp": peer(step + 1)}, device_id_type=MESH)

    each(count - 1, greet)
    pl.semaphore_signal(barrier, inc=1, device_id={"var": 1 - var}, device_id_type=MESH)

    def remote(source, target, ssem, rsem, owner):
        return pltpu.make_async_remote_copy(
            src_ref=source, dst_ref=target, send_sem=ssem, recv_sem=rsem,
            device_id={"samp": owner}, device_id_type=MESH,
        )

    def send(source, target, ssem, rsem, owner):
        return remote(source, target, ssem.at[owner], rsem.at[me], owner)

    def arrive(source, target, ssem, rsem, owner):
        remote(source, target, ssem.at[owner], rsem.at[owner], owner).wait_recv()

    def swap_with(source, target, ssem, rsem):
        return pltpu.make_async_remote_copy(
            src_ref=source, dst_ref=target, send_sem=ssem, recv_sem=rsem,
            device_id={"var": 1 - var}, device_id_type=MESH,
        )

    ids_row = codes[0:1, :].astype(F32)
    down_ranks = lax.broadcasted_iota(jnp.int32, (rows, rows), 0)
    along_ranks = lax.broadcasted_iota(jnp.int32, (rows, rows), 1)
    ids = jnp.sum(jnp.where(down_ranks == along_ranks, ids_row, 0.0), axis=1, keepdims=True)
    owner_row = jnp.zeros_like(ids_row)
    owner_of = jnp.zeros_like(ids)
    for owner in range(1, count):
        owner_row += jnp.where(ids_row >= owner * rows, 1.0, 0.0)
        owner_of += jnp.where(ids >= owner * rows, 1.0, 0.0)
    before = jnp.sum(
        jnp.where((owner_row == owner_of) & (along_ranks < down_ranks), 1.0, 0.0), axis=1, keepdims=True
    )
    key = (owner_of * width + before).astype(jnp.int32)
    place = (ids - owner_of * rows).astype(jnp.int32)
    ranks = lax.broadcasted_iota(jnp.int32, (rows, width), 0)
    lane = lax.broadcasted_iota(jnp.int32, (rows, width), 1)
    for owner in range(count):
        match = key == lane + owner * width
        place_out[owner] = jnp.max(jnp.where(match, place, -1), axis=0, keepdims=True)
        spot[owner] = jnp.max(jnp.where(match, ranks, -1), axis=0, keepdims=True)

    line = lax.broadcasted_iota(jnp.int32, (8, rows), 0)
    code = codes[1:2, :]
    labels = jnp.where(line == 0, code // 2, jnp.where(line == 1, code % 2, 0)).astype(F32)
    same = lax.broadcasted_iota(jnp.int32, (columns, columns), 0) == lax.broadcasted_iota(
        jnp.int32, (columns, columns), 1
    )
    pace = jnp.sum(jnp.where(same, step_row[...], 0.0), axis=1, keepdims=True)
    threshold = pace * jnp.sum(jnp.where(same, penalty_row[...], 0.0), axis=1, keepdims=True)
    column_fold = lax.rem(lax.broadcasted_iota(jnp.int32, (few, rows), 0) + var * few, FOLDS).astype(F32)
    mask[...] = jnp.where(labels[0:1, :] != column_fold, 1.0, 0.0)
    kept[...] = mask[...] * labels[1:2, :]
    place_in[me] = place_out[me]

    pl.semaphore_wait(barrier, count)

    def push_p(step):
        owner = peer(step + 1)
        send(place_out.at[owner], place_in.at[me], p_ss, p_rs, owner).start()
    each(count - 1, push_p)

    coef_load.wait()
    low[...] = coef[...].astype(BF16)
    shard[...] = coef[:, piece(me)]

    def arrange():
        block = jnp.zeros((rows, width), jnp.int32)

        def land_p(step):
            owner = peer(step + 1)
            arrive(place_out.at[owner], place_in.at[owner], p_ss, p_rs, owner)
            send(place_out.at[owner], place_in.at[me], p_ss, p_rs, owner).wait_send()
        each(count - 1, land_p)
        for owner in range(1, count):
            block += jnp.where(place_in[owner] == ranks, owner, 0)
        block = jnp.broadcast_to(jnp.sum(block, axis=1, keepdims=True), (rows, width))
        in_totals = (lane - share) == block
        for owner in range(count):
            span = slice(owner * width, (owner + 1) * width)
            hit = place_in[owner] == ranks
            to_time[:, span] = jnp.where(hit | in_totals, 1.0, 0.0).astype(BF16)
            to_id[:, span] = jnp.where(hit | ((lane == share) & (block > owner)), 1.0, 0.0).astype(BF16)
        spread = jnp.dot(labels.astype(BF16), to_time[...], preferred_element_type=F32)
        for owner in range(count):
            code_out[owner] = spread[:, owner * width:(owner + 1) * width]

        def push_l(step):
            owner = peer(step + 1)
            send(code_out.at[owner], code_in.at[me], l_ss, l_rs, owner).start()
        each(count - 1, push_l)
        code_in[me] = code_out[me]

    def sums():
        place_line = lax.broadcasted_iota(jnp.int32, (1, width), 1)
        for owner in range(count):
            span = slice(owner * width, (owner + 1) * width)
            beyond = (place_line >= share + me + 1) & (place_line < share + count)
            reach = jnp.where(beyond, rows, spot[owner])
            back = jnp.where(place_line == share, rows, spot[owner])
            later[:, span] = jnp.where(reach >= ranks, 1.0, 0.0).astype(BF16)
            earlier[:, span] = jnp.where(back >= ranks, 1.0, 0.0).astype(BF16)

    def time_labels():
        def land_l(step):
            owner = peer(step + 1)
            arrive(code_out.at[owner], code_in.at[owner], l_ss, l_rs, owner)
            send(code_out.at[owner], code_in.at[me], l_ss, l_rs, owner).wait_send()
        each(count - 1, land_l)
        labels_time = jnp.zeros((labels.shape[0], rows), F32)
        for owner in range(count):
            labels_time += across(
                code_in[owner].astype(BF16), jnp.where(spot[owner] == ranks, 1.0, 0.0).astype(BF16)
            )
        kept_time[...] = jnp.where(labels_time[0:1, :] != column_fold, 1.0, 0.0) * labels_time[1:2, :]

    def low_out_of(hop, number):
        part_of = low.at[band(number, CUTS_LOW), piece(me)]
        owner = me + side if hop is None else down(hop)
        index = (0 if hop is None else hop, number)
        return remote(part_of, part_of, c_ss.at[index], c_rs.at[index], owner)

    def low_relay(hop, number):
        part_of = low.at[band(number, CUTS_LOW), piece(up(hop))]
        return remote(part_of, part_of, fwd_ss.at[hop, number], fwd_rs.at[hop, number], me + side)

    def change_own(hop, number):
        index = (0 if hop is None else hop, number)
        bands = band(number, CUTS_LAST)
        source = change.at[bands, piece(me)]
        target = change_out.at[bands, piece(me)] if hop is None else source
        owner = me + side if hop is None else down(hop)
        return remote(source, target, f_ss.at[index], f_rs.at[index], owner)

    def change_relay(hop, number):
        bands = band(number, CUTS_LAST)
        return remote(
            change.at[bands, piece(up(hop))], change_out.at[bands, piece(up(hop))],
            last_ss.at[hop, number], last_rs.at[hop, number], me + side,
        )

    def change_keep(hop):
        owner = up(hop)
        return pltpu.make_async_copy(change.at[:, piece(owner)], change_out.at[:, piece(owner)], change_sem.at[hop])

    def send_y(hop, number):
        bands = band(number, CUTS_SUM)
        return remote(
            out_y.at[hop, bands, :], in_y.at[hop, bands, :], y_ss.at[hop, number], y_rs.at[hop, number], me + side
        )

    def send_z(hop, number):
        bands = band(number, CUTS_SUM)
        return remote(
            out_z.at[hop, bands, :], in_z.at[hop, bands, :], z_ss.at[hop, number], z_rs.at[hop, number], down(hop)
        )

    def add_part(owner):
        pred[...] += across(low[:, piece(owner)], geno[:, piece(owner)])

    def one_step(turn, first):
        if first:
            pred[...] = jnp.zeros_like(pred)

            def add_block(owner):
                block_load(owner).wait()
                add_part(owner)
            each(count, add_block)
        else:
            pred[...] = across(low[:, piece(me)], geno[:, piece(me)])
            for number in range(CUTS_LOW):
                low_out_of(None, number).wait_recv()
            add_part(me + side)

            def pass_on(hop):
                for number in range(CUTS_LOW):
                    low_out_of(hop, number).wait_recv()
                    low_relay(hop, number).start()
            hops(pass_on)
            hops(lambda hop: add_part(up(hop)))

            def add_side(hop):
                for number in range(CUTS_LOW):
                    low_relay(hop, number).wait_recv()
                add_part(up(hop) + side)
            hops(add_side)

        half_send[...] = pred[theirs, :]
        slot = lax.rem(turn, 2)
        swap = swap_with(half_send, half_recv.at[slot], half_ss, half_rs.at[slot])
        swap.start()
        if first:
            arrange()
        else:
            for number in range(CUTS_LOW):
                low_out_of(None, number).wait_send()

                def low_done(hop):
                    low_out_of(hop, number).wait_send()
                    low_relay(hop, number).wait_send()
                hops(low_done)
        swap.wait()

        weight = mask[...] * jnp.exp((pred[mine, :] + half_recv[slot]) * scale_vars)
        held[...] = weight
        spread = dot2(weight, to_time[...])
        for owner in range(count):
            out_a[owner] = spread[:, owner * width:(owner + 1) * width]

        def push_a(step):
            owner = peer(step + 1)
            send(out_a.at[owner], in_a.at[me], a_ss, a_rs, owner).start()
        each(count - 1, push_a)
        if first:
            sums()
            time_labels()
        risk = across2(out_a[me], later[:, slots(me)])
        for step in range(count - 1):
            owner = peer(step + 1)
            arrive(out_a.at[owner], in_a.at[owner], a_ss, a_rs, owner)
            risk += across2(in_a[owner], later[:, slots(owner)])
        events = kept_time[...]
        ratio = events / jnp.where(events > 0, risk, 1.0)
        spread = dot2(ratio, earlier[...])
        for owner in range(count):
            out_b[owner] = spread[:, owner * width:(owner + 1) * width]

        def push_b(step):
            owner = peer(step + 1)
            send(out_b.at[owner], in_b.at[me], b_ss, b_rs, owner).start()
        each(count - 1, push_b)
        hazard = across2(out_b[me], to_id[:, slots(me)])
        for step in range(count - 1):
            owner = peer(step + 1)
            arrive(out_b.at[owner], in_b.at[owner], b_ss, b_rs, owner)
            hazard += across2(in_b[owner], to_id[:, slots(owner)])
        score[mine, :] = (held[...] * hazard - kept[...]).astype(BF16)
        trade = swap_with(score.at[mine, :], score.at[mine, :], s_ss, s_rs)
        trade.start()
        trade.wait()

        def product(owner):
            return jnp.dot(score[...], geno[:, piece(owner)], preferred_element_type=F32)

        def give(hop):
            out_y[hop] = product(down(hop) + side).astype(BF16)
            for number in range(CUTS_SUM):
                send_y(hop, number).start()

        def keep(hop):
            own_g[hop] = product(down(hop))

        hops(give)
        give(0)
        hops(keep)
        keep(0)

        def gather_pair(hop):
            for number in range(CUTS_SUM):
                bands = band(number, CUTS_SUM)
                send_y(hop, number).wait_recv()
                out_z[hop, bands, :] = (own_g[hop, bands, :] + in_y[hop, bands, :].astype(F32)).astype(BF16)
                send_z(hop, number).start()
        hops(gather_pair)
        for number in range(CUTS_SUM):
            send_y(0, number).wait_recv()
        shard_sum = own_g.at[0]
        shard_sum[...] += in_y[0].astype(F32)

        def gather_all(hop):
            for number in range(CUTS_SUM):
                send_z(hop, number).wait_recv()
            shard_sum[...] += in_z[hop].astype(F32)
        hops(gather_all)
        stepped = shard[...] - pace * (shard_sum[...] * scale_samples)
        shrunk = jnp.maximum(jnp.abs(stepped) - threshold, 0.0)
        fresh = jnp.where(stepped > 0, shrunk, -shrunk)
        shard[...] = fresh

        def spread_low():
            low[:, piece(me)] = fresh.astype(BF16)
            for number in range(CUTS_LOW):
                hops(lambda hop: low_out_of(hop, number).start())
                low_out_of(None, number).start()

        if first:
            spread_low()
        else:
            pl.when(turn < ITERS - 1)(spread_low)

        def drained(step):
            owner = peer(step + 1)
            send(out_a.at[owner], in_a.at[me], a_ss, a_rs, owner).wait_send()
            send(out_b.at[owner], in_b.at[me], b_ss, b_rs, owner).wait_send()
        each(count - 1, drained)

        def sent(hop):
            for number in range(CUTS_SUM):
                send_y(hop, number).wait_send()
                send_z(hop, number).wait_send()
        hops(sent)
        for number in range(CUTS_SUM):
            send_y(0, number).wait_send()

    one_step(0, True)
    lax.fori_loop(1, ITERS, lambda turn, carry: (one_step(turn, False), carry)[1], 0)

    change[:, piece(me)] = (shard[...] - low[:, piece(me)].astype(F32)).astype(BF16)
    for number in range(CUTS_LAST):
        hops(lambda hop: change_own(hop, number).start())
        change_own(None, number).start()
    own_keep = change_keep(0)
    own_keep.start()
    low_keep = pltpu.make_async_copy(low, low_out, end_sem.at[0])
    low_keep.start()
    score_wide[...] = score[...].astype(F32)
    score_keep = pltpu.make_async_copy(score_wide, score_out, end_sem.at[1])
    score_keep.start()

    def pass_change(number):
        def go(hop):
            change_own(hop, number).wait_recv()
            change_relay(hop, number).start()
            if number == CUTS_LAST - 1:
                change_keep(hop).start()
        hops(go)
    for number in range(CUTS_LAST):
        pass_change(number)
    own_keep.wait()
    low_keep.wait()
    score_keep.wait()

    def finish(hop):
        change_keep(hop).wait()
        for number in range(CUTS_LAST):
            change_own(hop, number).wait_send()
            change_relay(hop, number).wait()
    hops(finish)
    for number in range(CUTS_LAST):
        change_own(None, number).wait()


def local(genotypes, coefficients, time_order, fold_label, event_flag, penalty, step_size):
    rows = genotypes.shape[0]
    columns, variants = coefficients.shape
    count = lax.axis_size("samp")
    half = count // 2
    share = rows // count
    width = -(-(share + count) // 128) * 128
    total = count * width
    part = variants // count
    few = columns // 2

    codes = jnp.stack([time_order, fold_label * 2 + event_flag])
    vmem = pl.BlockSpec(memory_space=pltpu.VMEM)
    away = pl.BlockSpec(memory_space=pl.ANY)
    dma = pltpu.SemaphoreType.DMA
    low, change, score = pl.pallas_call(
        functools.partial(path_kernel, count, 1.0 / math.sqrt(VARS), 1.0 / math.sqrt(rows * count)),
        out_shape=(
            jax.ShapeDtypeStruct((columns, variants), BF16),
            jax.ShapeDtypeStruct((columns, variants), BF16),
            jax.ShapeDtypeStruct((columns, rows), F32),
        ),
        in_specs=[away] * 2 + [vmem] * 3,
        out_specs=(away, away, away),
        scratch_shapes=[
            pltpu.VMEM((rows, variants), BF16),
            pltpu.VMEM((columns, variants), F32),
            pltpu.VMEM((rows, total), BF16),
            pltpu.VMEM((rows, total), BF16),
            pltpu.VMEM((rows, total), BF16),
            pltpu.VMEM((rows, total), BF16),
            pltpu.VMEM((few, rows), F32),
            pltpu.VMEM((few, rows), F32),
            pltpu.VMEM((few, rows), F32),
            pltpu.VMEM((count, 1, width), jnp.int32),
            pltpu.VMEM((count, 1, width), jnp.int32),
            pltpu.VMEM((count, 1, width), jnp.int32),
            pltpu.VMEM((count, 8, width), F32),
            pltpu.VMEM((count, 8, width), F32),
            pltpu.VMEM((columns, variants), BF16),
            pltpu.VMEM((columns, variants), BF16),
            pltpu.VMEM((columns, part), F32),
            pltpu.VMEM((few, rows), F32),
            pltpu.VMEM((2, few, rows), F32),
            pltpu.VMEM((count, few, width), F32),
            pltpu.VMEM((count, few, width), F32),
            pltpu.VMEM((count, few, width), F32),
            pltpu.VMEM((count, few, width), F32),
            pltpu.VMEM((half, columns, part), BF16),
            pltpu.VMEM((half, columns, part), BF16),
            pltpu.VMEM((half, columns, part), BF16),
            pltpu.VMEM((half, columns, part), BF16),
            pltpu.VMEM((half, columns, part), F32),
            pltpu.VMEM((columns, rows), F32),
            pltpu.VMEM((few, rows), F32),
            pltpu.VMEM((columns, rows), BF16),
            pltpu.VMEM((columns, rows), F32),
            dma((count,)), dma, dma((2,)), dma((half,)),
            dma, dma, dma, dma((2,)),
        ] + [dma((count,))] * 8 + [dma((half, CUTS_SUM))] * 4 + [dma((half, CUTS_LOW))] * 4
        + [dma((half, CUTS_LAST))] * 4,
        compiler_params=pltpu.CompilerParams(
            collective_id=0, has_side_effects=True, vmem_limit_bytes=48 * 1024 * 1024
        ),
    )(genotypes, coefficients, codes, step_size[None], penalty[None])
    return low.astype(F32) + change.astype(F32), score.astype(BF16)


def solution(mesh):
    placed = (
        P("samp", "var"),
        P("pheno", "var"),
        P(("pheno", "samp")),
        P(("pheno", "samp")),
        P(("pheno", "samp")),
        P(),
        P(),
    )
    return jax.shard_map(
        local,
        mesh=mesh,
        in_specs=placed,
        out_specs=(P("pheno", "var"), P("pheno", "samp")),
        check_vma=False,
    )
```

time: 153 us -> 122 us (0.80)
  Pallas kernels: 143 us -> 116 us
  other arithmetic: 4.82 us -> 2.42 us
    pallas_call x1, Pallas kernels: 143 us -> 116 us  [local(): pl.pallas_call(functools.partial(path_kernel, count, 1.0 / math.sqrt(VARS...]
    select_n x4 -> x0, other arithmetic: 2.61 us -> none  [the longest x1 0.7 us: local(): place = time_order % rows]
    unnamed x4 -> x6, local copies, waits for them, and re-layouts: 3.67 us -> 2.53 us
where the time goes in v1:
time: 122 us
  Pallas kernels  116 us (95%)
  local copies, waits for them, and re-layouts  3.22 us (3%)
  other arithmetic  2.42 us (2%)
    pallas_call x1, Pallas kernels, local(): pl.pallas_call(functools.partial(path_kernel, count, 1.0 / math.sqrt(VARS...  116 us
    unnamed x6, local copies, waits for them, and re-layouts  2.53 us

profile of v1, /device:TPU:0, one launch (start us, length us, event | category | flops | bytes accessed | tf_op | source)
XLA Modules:
  0.0 122.2 jit_solution(14630460440700655703)
XLA Ops:
  0.6 0.7 stack.9
  1.3 0.7 multiply_add_fusion
  2.0 0.0 copy-start
  2.1 1.2 copy-done
  3.3 0.0 copy-start.1
  3.3 0.7 copy-done.1
  3.9 0.0 copy-start.2
  3.9 0.7 copy-done.2
  4.6 115.9 %shard_map.86 = (bf16[32,8192]{1,0:T(8,128)(2,1)S(1)}, bf16[32,8192]{1,0:T(8,128)(2,1)S(1)}, f32[32,576]{1,0:T(8,128)S(1)}) custom-call(bf16[576,8192]{1,0:T(8,128)(2,1)} %geno_in.1, f32[32,8192]{1,0:T(8,128)S(1)} %copy-done, s32[2,576]{1,0:T(2,128)S(1)} %pad_add_fusion.codes, f32[1,32]{1,0:T(1,128)S(1)} %bitcast.2, f32[1,32]{1,0:T(1,128)S(1)} %bitcast.3), custom_call_target="tpu_custom_call" | custom-call | tf_op jit(solution)/shard_map/pallas_call | solution.py:470
  120.5 1.1 convert_add_fusion
  121.6 0.6 convert_element_type.11
  (2 shorter events, 0.0 us)
Async XLA Ops:
  2.0 1.2 %copy-start = (f32[32,8192]{1,0:T(8,128)S(1)}, f32[32,8192]{1,0:T(8,128)}, u32[]{:S(2)}) copy-start(f32[32,8192]{1,0:T(8,128)} %coef_in.1) | copy-start | bytes 3145732
  3.3 0.7 copy-start.1
  3.9 0.7 copy-start.2

commit v2 on v1

v2 whole, which is shorter than its diff:
```python
import functools
import math

import jax
import jax.numpy as jnp
from jax import lax
from jax.experimental import pallas as pl
from jax.experimental.pallas import tpu as pltpu
from jax.sharding import PartitionSpec as P

VARS = 16384
FOLDS = 8
ITERS = 3
MESH = pl.DeviceIdType.MESH
F32 = jnp.float32
BF16 = jnp.bfloat16


def each(count, body):
    if count <= 8:
        for step in range(count):
            body(step)
    else:
        lax.fori_loop(0, count, lambda step, carry: (body(step), carry)[1], 0)


def halves(value):
    high = value.astype(BF16)
    low = (value - high.astype(F32)).astype(BF16)
    return jnp.concatenate([high, low], axis=0)


def across(left, right):
    return lax.dot_general(left, right, (((1,), (1,)), ((), ())), preferred_element_type=F32)


def across2(value, matrix):
    rows = value.shape[0]
    both = across(halves(value), matrix)
    return both[:rows] + both[rows:]


def dot2(value, matrix):
    rows = value.shape[0]
    both = jnp.dot(halves(value), matrix, preferred_element_type=F32)
    return both[:rows] + both[rows:]


def path_kernel(
    count, scale_vars, scale_samples,
    geno_in, coef_in, facts,
    low_out, change_out, score_out,
    geno, coef, to_time, later, earlier, to_id, mask, kept, kept_time, place_out, place_in, spot, code_out, code_in,
    low, change, shard, pace, threshold, half_recv, out_a, in_a, out_b, in_b,
    out_y, in_y, out_z, in_z, own_g, pred, held, score, score_wide,
    geno_sem, coef_sem, end_sem, keep_sem, s_ss, s_rs, half_ss, half_rs, p_ss, l_ss, a_ss, b_ss, y_ss, z_ss,
    p_rs, l_rs, a_rs, b_rs, y_rs, z_rs, c_ss, c_rs, fwd_ss, fwd_rs,
):
    me = lax.axis_index("samp")
    var = lax.axis_index("var")
    columns, variants = coef.shape
    rows = geno.shape[0]
    part = variants // count
    width = later.shape[1] // count
    share = rows // count
    half = count // 2
    few = columns // 2
    side = 1 - 2 * lax.rem(me, 2)

    def peer(step):
        return lax.rem(me + step, count)

    def down(hop):
        return lax.rem(me + 2 * hop, count)

    def up(hop):
        return lax.rem(me + count - 2 * hop, count)

    def piece(owner):
        return pl.ds(pl.multiple_of(owner * part, part), part)

    def hops(body):
        if half <= 8:
            for hop in sorted(range(1, half), key=lambda hop: (abs(2 * hop - half), hop)):
                body(hop)
        else:
            lax.fori_loop(1, half, lambda hop, carry: (body(hop), carry)[1], 0)

    def slots(owner):
        return pl.ds(pl.multiple_of(owner * width, width), width)

    def block_load(owner):
        return pltpu.make_async_copy(geno_in.at[:, piece(owner)], geno.at[:, piece(owner)], geno_sem.at[owner])

    coef_load = pltpu.make_async_copy(coef_in, coef, coef_sem)
    coef_load.start()
    each(count, lambda owner: block_load(owner).start())

    barrier = pltpu.get_barrier_semaphore()

    def greet(step):
        pl.semaphore_signal(barrier, inc=1, device_id={"samp": peer(step + 1)}, device_id_type=MESH)

    each(count - 1, greet)
    pl.semaphore_signal(barrier, inc=1, device_id={"var": 1 - var}, device_id_type=MESH)

    def remote(source, target, ssem, rsem, owner):
        return pltpu.make_async_remote_copy(
            src_ref=source, dst_ref=target, send_sem=ssem, recv_sem=rsem,
            device_id={"samp": owner}, device_id_type=MESH,
        )

    def scatter(source, target, ssem, rsem):
        def push(step):
            owner = peer(step + 1)
            remote(source.at[owner], target.at[me], ssem, rsem.at[me], owner).start()
        each(count - 1, push)

    def arrive(target, rsem, owner):
        remote(target.at[owner], target.at[owner], rsem.at[owner], rsem.at[owner], owner).wait_recv()

    def scattered(source, ssem):
        most = source.at[pl.ds(0, count - 1)]
        remote(most, most, ssem, ssem, me + side).wait_send()

    def swap_with(source, target, ssem, rsem):
        return pltpu.make_async_remote_copy(
            src_ref=source, dst_ref=target, send_sem=ssem, recv_sem=rsem,
            device_id={"var": 1 - var}, device_id_type=MESH,
        )

    ids_row = facts[0:1, :]
    down_ranks = lax.broadcasted_iota(jnp.int32, (rows, rows), 0)
    along_ranks = lax.broadcasted_iota(jnp.int32, (rows, rows), 1)
    ids = jnp.sum(jnp.where(down_ranks == along_ranks, ids_row, 0.0), axis=1, keepdims=True)
    owner_row = jnp.zeros_like(ids_row)
    owner_of = jnp.zeros_like(ids)
    for owner in range(1, count):
        owner_row += jnp.where(ids_row >= owner * rows, 1.0, 0.0)
        owner_of += jnp.where(ids >= owner * rows, 1.0, 0.0)
    before = jnp.sum(
        jnp.where((owner_row == owner_of) & (along_ranks < down_ranks), 1.0, 0.0), axis=1, keepdims=True
    )
    key = (owner_of * width + before).astype(jnp.int32)
    place = (ids - owner_of * rows).astype(jnp.int32)
    ranks = lax.broadcasted_iota(jnp.int32, (rows, width), 0)
    lane = lax.broadcasted_iota(jnp.int32, (rows, width), 1)
    for owner in range(count):
        match = key == lane + owner * width
        place_out[owner] = jnp.max(jnp.where(match, place, -1), axis=0, keepdims=True)
        spot[owner] = jnp.max(jnp.where(match, ranks, -1), axis=0, keepdims=True)

    line = lax.broadcasted_iota(jnp.int32, (8, rows), 0)
    labels = jnp.where(line == 0, facts[1:2, :], jnp.where(line == 1, facts[2:3, :], 0.0))
    same = lax.broadcasted_iota(jnp.int32, (columns, columns), 0) == lax.broadcasted_iota(
        jnp.int32, (columns, columns), 1
    )
    step_size = jnp.sum(jnp.where(same, facts[3:4, :columns], 0.0), axis=1, keepdims=True)
    least = step_size * jnp.sum(jnp.where(same, facts[4:5, :columns], 0.0), axis=1, keepdims=True)
    column_fold = lax.rem(lax.broadcasted_iota(jnp.int32, (columns, rows), 0), FOLDS).astype(F32)
    trained = jnp.where(labels[0:1, :] != column_fold, 1.0, 0.0)
    counted = trained * labels[1:2, :]
    for group in range(2):
        span = slice(group * few, (group + 1) * few)
        pace[group] = step_size[span]
        threshold[group] = least[span]
        mask[group] = trained[span]
        kept[group] = counted[span]
    place_in[me] = place_out[me]

    pl.semaphore_wait(barrier, count)
    scatter(place_out, place_in, p_ss, p_rs)

    coef_load.wait()
    for group in range(2):
        low[group] = coef[group * few:(group + 1) * few, :].astype(BF16)
        shard[group] = coef[group * few:(group + 1) * few, piece(me)]

    def arrange():
        block = jnp.zeros((rows, width), jnp.int32)
        each(count - 1, lambda step: arrive(place_in, p_rs, peer(step + 1)))
        scattered(place_out, p_ss)
        for owner in range(1, count):
            block += jnp.where(place_in[owner] == ranks, owner, 0)
        block = jnp.broadcast_to(jnp.sum(block, axis=1, keepdims=True), (rows, width))
        in_totals = (lane - share) == block
        for owner in range(count):
            span = slice(owner * width, (owner + 1) * width)
            hit = place_in[owner] == ranks
            to_time[:, span] = jnp.where(hit | in_totals, 1.0, 0.0).astype(BF16)
            to_id[:, span] = jnp.where(hit | ((lane == share) & (block > owner)), 1.0, 0.0).astype(BF16)
        spread = jnp.dot(labels.astype(BF16), to_time[...], preferred_element_type=F32)
        for owner in range(count):
            code_out[owner] = spread[:, owner * width:(owner + 1) * width]
        scatter(code_out, code_in, l_ss, l_rs)
        code_in[me] = code_out[me]

    def sums():
        place_line = lax.broadcasted_iota(jnp.int32, (1, width), 1)
        for owner in range(count):
            span = slice(owner * width, (owner + 1) * width)
            beyond = (place_line >= share + me + 1) & (place_line < share + count)
            reach = jnp.where(beyond, rows, spot[owner])
            back = jnp.where(place_line == share, rows, spot[owner])
            later[:, span] = jnp.where(reach >= ranks, 1.0, 0.0).astype(BF16)
            earlier[:, span] = jnp.where(back >= ranks, 1.0, 0.0).astype(BF16)

    def time_labels():
        each(count - 1, lambda step: arrive(code_in, l_rs, peer(step + 1)))
        scattered(code_out, l_ss)
        labels_time = jnp.zeros((labels.shape[0], rows), F32)
        for owner in range(count):
            labels_time += across(
                code_in[owner].astype(BF16), jnp.where(spot[owner] == ranks, 1.0, 0.0).astype(BF16)
            )
        counted_time = jnp.where(labels_time[0:1, :] != column_fold, 1.0, 0.0) * labels_time[1:2, :]
        for group in range(2):
            kept_time[group] = counted_time[group * few:(group + 1) * few]

    def tell(held_in, hop, band, group):
        block = held_in.at[group, :, piece(me)]
        owner = me + side if hop is None else down(hop)
        index = (0 if hop is None else hop, band)
        return remote(block, block, c_ss.at[index], c_rs.at[index], owner)

    def relay(held_in, end, hop, band, group):
        span = piece(up(hop))
        return remote(
            held_in.at[group, :, span], end.at[group, :, span], fwd_ss.at[hop, band], fwd_rs.at[hop, band], me + side
        )

    def tell_all(held_in, band, group):
        hops(lambda hop: tell(held_in, hop, band, group).start())
        tell(held_in, None, band, group).start()

    def pass_on(held_in, end, band, group):
        def go(hop):
            tell(held_in, hop, band, group).wait_recv()
            relay(held_in, end, hop, band, group).start()
        hops(go)

    def told(held_in, end, band, group):
        def go(hop):
            tell(held_in, hop, band, group).wait_send()
            relay(held_in, end, hop, band, group).wait_send()
        hops(go)
        tell(held_in, None, band, group).wait_send()

    def send_y(hop, band):
        return remote(out_y.at[hop, band], in_y.at[hop, band], y_ss, y_rs.at[hop, band], me + side)

    def send_z(hop, band):
        return remote(out_z.at[hop, band], in_z.at[hop, band], z_ss, z_rs.at[hop, band], down(hop))

    def add_part(owner, group):
        pred[group] += across(low[group, :, piece(owner)], geno[:, piece(owner)])

    def one_step(turn, first):
        own = lax.rem(var + turn, 2)
        other = 1 - own
        slot = lax.rem(turn, 2)
        swap = swap_with(pred.at[other], half_recv.at[slot], half_ss, half_rs.at[slot])
        if first:
            pred[...] = jnp.zeros_like(pred)

            def add_block(owner):
                block_load(owner).wait()
                both = across(low[:, :, piece(owner)].reshape(columns, part), geno[:, piece(owner)])
                pred[...] += both.reshape(2, few, rows)
            each(count, add_block)
            swap.start()
            arrange()
        else:
            def begin(band, group):
                pred[group] = across(low[group, :, piece(me)], geno[:, piece(me)])
                tell(low, None, band, group).wait_recv()
                add_part(me + side, group)

            def add_side(band, group):
                def go(hop):
                    relay(low, low, hop, band, group).wait_recv()
                    add_part(up(hop) + side, group)
                hops(go)

            begin(0, other)
            pass_on(low, low, 0, other)
            begin(1, own)
            hops(lambda hop: add_part(up(hop), other))
            pass_on(low, low, 1, own)
            add_side(0, other)
            swap.start()
            hops(lambda hop: add_part(up(hop), own))
            add_side(1, own)
            told(low, low, 0, other)
            told(low, low, 1, own)
        swap.wait()

        weight = mask[own] * jnp.exp((pred[own] + half_recv[slot]) * scale_vars)
        held[...] = weight
        spread = dot2(weight, to_time[...])
        for owner in range(count):
            out_a[owner] = spread[:, owner * width:(owner + 1) * width]
        scatter(out_a, in_a, a_ss, a_rs)
        if first:
            sums()
            time_labels()
        risk = across2(out_a[me], later[:, slots(me)])
        for step in range(count - 1):
            owner = peer(step + 1)
            arrive(in_a, a_rs, owner)
            risk += across2(in_a[owner], later[:, slots(owner)])
        events = kept_time[own]
        ratio = events / jnp.where(events > 0, risk, 1.0)
        spread = dot2(ratio, earlier[...])
        for owner in range(count):
            out_b[owner] = spread[:, owner * width:(owner + 1) * width]
        scatter(out_b, in_b, b_ss, b_rs)
        hazard = across2(out_b[me], to_id[:, slots(me)])
        for step in range(count - 1):
            owner = peer(step + 1)
            arrive(in_b, b_rs, owner)
            hazard += across2(in_b[owner], to_id[:, slots(owner)])
        score[own] = (held[...] * hazard - kept[own]).astype(BF16)
        trade = swap_with(score.at[own], score.at[own], s_ss, s_rs)
        trade.start()

        def product(left, owner):
            return jnp.dot(left, geno[:, piece(owner)], preferred_element_type=F32)

        def give(band, group):
            def go(hop):
                out_y[hop, band] = product(score[group], down(hop) + side).astype(BF16)
                send_y(hop, band).start()
            hops(go)
            go(0)

        def keep(hop):
            own_g[hop] = product(score[...].reshape(columns, rows), down(hop)).reshape(2, few, part)

        give(0, own)
        trade.wait()
        give(1, other)
        hops(keep)
        keep(0)

        def pairs(band, group):
            def go(hop):
                send_y(hop, band).wait_recv()
                out_z[hop, band] = (own_g[hop, group] + in_y[hop, band].astype(F32)).astype(BF16)
                send_z(hop, band).start()
            hops(go)

        def update(band, group):
            total = own_g.at[0, group]
            send_y(0, band).wait_recv()
            total[...] += in_y[0, band].astype(F32)

            def go(hop):
                send_z(hop, band).wait_recv()
                total[...] += in_z[hop, band].astype(F32)
            hops(go)
            stepped = shard[group] - pace[group] * (total[...] * scale_samples)
            shrunk = jnp.maximum(jnp.abs(stepped) - threshold[group], 0.0)
            fresh = jnp.where(stepped > 0, shrunk, -shrunk)
            shard[group] = fresh

            def spread_low():
                low[group, :, piece(me)] = fresh.astype(BF16)
                tell_all(low, band, group)

            def spread_change():
                change[group, :, piece(me)] = (fresh - low[group, :, piece(me)].astype(F32)).astype(BF16)
                tell_all(change, band, group)

            if first:
                spread_low()
            else:
                pl.when(turn < ITERS - 1)(spread_low)
                pl.when(turn == ITERS - 1)(spread_change)

        pairs(0, own)
        pairs(1, other)
        update(0, own)
        update(1, other)
        scattered(out_a, a_ss)
        scattered(out_b, b_ss)
        remote(out_y, out_y, y_ss, y_ss, me + side).wait_send()
        most = out_z.at[pl.ds(1, half - 1)]
        remote(most, most, z_ss, z_ss, me + side).wait_send()

    one_step(0, True)
    lax.fori_loop(1, ITERS, lambda turn, carry: (one_step(turn, False), carry)[1], 0)

    def change_keep(hop):
        span = piece(up(hop))
        return pltpu.make_async_copy(change.at[:, :, span], change_out.at[:, :, span], keep_sem.at[hop])

    def side_keep():
        span = piece(me + side)
        return pltpu.make_async_copy(change.at[:, :, span], change_out.at[:, :, span], end_sem.at[2])

    own = lax.rem(var + ITERS - 1, 2)
    change_keep(0).start()
    low_keep = pltpu.make_async_copy(low, low_out, end_sem.at[0])
    low_keep.start()
    score_wide[...] = score[...].astype(F32)
    score_keep = pltpu.make_async_copy(score_wide, score_out, end_sem.at[1])
    score_keep.start()
    pass_on(change, change_out, 0, own)
    pass_on(change, change_out, 1, 1 - own)
    hops(lambda hop: change_keep(hop).start())
    tell(change, None, 0, own).wait_recv()
    tell(change, None, 1, 1 - own).wait_recv()
    side_keep().start()
    told(change, change_out, 0, own)
    told(change, change_out, 1, 1 - own)
    low_keep.wait()
    score_keep.wait()
    change_keep(0).wait()
    hops(lambda hop: change_keep(hop).wait())
    side_keep().wait()
    hops(lambda hop: relay(change, change_out, hop, 0, own).wait_recv())
    hops(lambda hop: relay(change, change_out, hop, 1, 1 - own).wait_recv())


def local(genotypes, coefficients, time_order, fold_label, event_flag, penalty, step_size):
    rows = genotypes.shape[0]
    columns, variants = coefficients.shape
    count = lax.axis_size("samp")
    half = count // 2
    share = rows // count
    width = -(-(share + count) // 128) * 128
    total = count * width
    part = variants // count
    few = columns // 2

    def padded(value):
        return jnp.pad(value, (0, rows - columns))

    facts = jnp.stack([
        time_order.astype(F32), fold_label.astype(F32), event_flag.astype(F32), padded(step_size), padded(penalty),
    ])
    vmem = pl.BlockSpec(memory_space=pltpu.VMEM)
    away = pl.BlockSpec(memory_space=pl.ANY)
    dma = pltpu.SemaphoreType.DMA
    low, change, score = pl.pallas_call(
        functools.partial(path_kernel, count, 1.0 / math.sqrt(VARS), 1.0 / math.sqrt(rows * count)),
        out_shape=(
            jax.ShapeDtypeStruct((2, few, variants), BF16),
            jax.ShapeDtypeStruct((2, few, variants), BF16),
            jax.ShapeDtypeStruct((2, few, rows), F32),
        ),
        in_specs=[away] * 2 + [vmem],
        out_specs=(away, away, away),
        scratch_shapes=[
            pltpu.VMEM((rows, variants), BF16),
            pltpu.VMEM((columns, variants), F32),
            pltpu.VMEM((rows, total), BF16),
            pltpu.VMEM((rows, total), BF16),
            pltpu.VMEM((rows, total), BF16),
            pltpu.VMEM((rows, total), BF16),
            pltpu.VMEM((2, few, rows), F32),
            pltpu.VMEM((2, few, rows), F32),
            pltpu.VMEM((2, few, rows), F32),
            pltpu.VMEM((count, 1, width), jnp.int32),
            pltpu.VMEM((count, 1, width), jnp.int32),
            pltpu.VMEM((count, 1, width), jnp.int32),
            pltpu.VMEM((count, 8, width), F32),
            pltpu.VMEM((count, 8, width), F32),
            pltpu.VMEM((2, few, variants), BF16),
            pltpu.VMEM((2, few, variants), BF16),
            pltpu.VMEM((2, few, part), F32),
            pltpu.VMEM((2, few, 1), F32),
            pltpu.VMEM((2, few, 1), F32),
            pltpu.VMEM((2, few, rows), F32),
            pltpu.VMEM((count, few, width), F32),
            pltpu.VMEM((count, few, width), F32),
            pltpu.VMEM((count, few, width), F32),
            pltpu.VMEM((count, few, width), F32),
            pltpu.VMEM((half, 2, few, part), BF16),
            pltpu.VMEM((half, 2, few, part), BF16),
            pltpu.VMEM((half, 2, few, part), BF16),
            pltpu.VMEM((half, 2, few, part), BF16),
            pltpu.VMEM((half, 2, few, part), F32),
            pltpu.VMEM((2, few, rows), F32),
            pltpu.VMEM((few, rows), F32),
            pltpu.VMEM((2, few, rows), BF16),
            pltpu.VMEM((2, few, rows), F32),
            dma((count,)), dma, dma((3,)), dma((half,)),
            dma, dma, dma, dma((2,)),
        ] + [dma] * 6 + [dma((count,))] * 4 + [dma((half, 2))] * 6,
        compiler_params=pltpu.CompilerParams(
            collective_id=0, has_side_effects=True, vmem_limit_bytes=60 * 1024 * 1024
        ),
    )(genotypes, coefficients, facts)
    coefs = low.astype(F32) + change.astype(F32)
    return coefs.reshape(columns, variants), score.astype(BF16).reshape(columns, rows)


def solution(mesh):
    placed = (
        P("samp", "var"),
        P("pheno", "var"),
        P(("pheno", "samp")),
        P(("pheno", "samp")),
        P(("pheno", "samp")),
        P(),
        P(),
    )
    return jax.shard_map(
        local,
        mesh=mesh,
        in_specs=placed,
        out_specs=(P("pheno", "var"), P("pheno", "samp")),
        check_vma=False,
    )
```

time: 122 us -> 119 us (0.975)
  Pallas kernels: 116 us -> 110 us
  other arithmetic: 2.42 us -> 5.85 us
  local copies, waits for them, and re-layouts: 3.22 us -> 1.97 us
    pallas_call x1, Pallas kernels: 116 us -> 110 us  [local(): pl.pallas_call(functools.partial(path_kernel, count, 1.0 / math.sqrt(VARS...]
    convert_element_type x1 -> x4, other arithmetic: 0.62 us -> 3.58 us  [the longest x1 1.51 us: local(): score.astype(BF16).reshape(columns, rows)]
    unnamed x6 -> x0, local copies, waits for them, and re-layouts: 2.53 us -> none
    pad x0 -> x2, local copies, waits for them, and re-layouts: none -> 1.32 us  [padded(): return jnp.pad(value, (0, rows - columns))]
where the time goes in v2:
time: 119 us; the launch traced here: 118 us
  Pallas kernels  110 us (92%)
  other arithmetic  5.85 us (5%)
  local copies, waits for them, and re-layouts  1.97 us (2%)
    pallas_call x1, Pallas kernels, local(): pl.pallas_call(functools.partial(path_kernel, count, 1.0 / math.sqrt(VARS...  110 us

profile of v2, /device:TPU:0, one launch (start us, length us, event | category | flops | bytes accessed | tf_op | source)
XLA Modules:
  0.0 118.5 jit_solution(8185752793569503147)
XLA Ops:
  0.6 0.7 convert_element_type.21
  1.3 0.7 convert_element_type.22
  2.0 0.7 convert_element_type.23
  2.7 0.7 pad.8
  3.4 0.7 pad.7
  4.0 0.6 stack.23.facts
  4.7 110.0 %shard_map.86 = (bf16[2,16,8192]{2,1,0:T(8,128)(2,1)}, bf16[2,16,8192]{2,1,0:T(8,128)(2,1)}, f32[2,16,576]{2,1,0:T(8,128)}) custom-call(bf16[576,8192]{1,0:T(8,128)(2,1)} %geno_in.1, f32[32,8192]{1,0:T(8,128)} %coef_in.1, f32[5,576]{1,0:T(8,128)} %stack.23.facts), custom_call_target="tpu_custom_call" | custom-call | tf_op jit(solution)/shard_map/pallas_call | solution.py:446
  114.7 2.3 %convert_add_fusion = f32[2,16,8192]{2,1,0:T(8,128)} fusion(bf16[2,16,8192]{2,1,0:T(8,128)(2,1)} %get-tuple-element.6, bf16[2,16,8192]{2,1,0:T(8,128)(2,1)} %get-tuple-element.5), kind=kLoop, calls=%fused_computation | loop fusion | flops 786432 | bytes 2097152 | tf_op jit(solution)/shard_map/add | solution.py:496
  117.0 1.5 %convert_element_type.26 = bf16[2,16,576]{2,1,0:T(8,128)(2,1)} convert(f32[2,16,576]{2,1,0:T(8,128)} %get-tuple-element.7) | non-fusion elementwise | flops 18432 | bytes 110592 | tf_op jit(solution)/shard_map/convert_element_type | solution.py:497
  (5 shorter events, 0.0 us)

commit v3 on v2

--- a/solution.py
+++ b/solution.py
@@ -10,6 +10,7 @@
 
 VARS = 16384
 FOLDS = 8
+CODES = 2 * FOLDS
 ITERS = 3
 MESH = pl.DeviceIdType.MESH
 F32 = jnp.float32
@@ -48,13 +49,13 @@
 
 def path_kernel(
     count, scale_vars, scale_samples,
-    geno_in, coef_in, facts,
+    geno_in, coef_in, codes, rates,
     low_out, change_out, score_out,
     geno, coef, to_time, later, earlier, to_id, mask, kept, kept_time, place_out, place_in, spot, code_out, code_in,
     low, change, shard, pace, threshold, half_recv, out_a, in_a, out_b, in_b,
     out_y, in_y, out_z, in_z, own_g, pred, held, score, score_wide,
-    geno_sem, coef_sem, end_sem, keep_sem, s_ss, s_rs, half_ss, half_rs, p_ss, l_ss, a_ss, b_ss, y_ss, z_ss,
-    p_rs, l_rs, a_rs, b_rs, y_rs, z_rs, c_ss, c_rs, fwd_ss, fwd_rs,
+    geno_sem, coef_sem, end_sem, s_ss, s_rs, half_ss, half_rs, p_ss, l_ss, a_ss, b_ss, y_ss, z_ss, c_ss, fwd_ss,
+    p_rs, l_rs, a_rs, b_rs, y_rs, z_rs, c_rs, fwd_rs,
 ):
     me = lax.axis_index("samp")
     var = lax.axis_index("var")
@@ -92,9 +93,14 @@
     def block_load(owner):
         return pltpu.make_async_copy(geno_in.at[:, piece(owner)], geno.at[:, piece(owner)], geno_sem.at[owner])
 
-    coef_load = pltpu.make_async_copy(coef_in, coef, coef_sem)
-    coef_load.start()
-    each(count, lambda owner: block_load(owner).start())
+    def coef_load(owner):
+        return pltpu.make_async_copy(coef_in.at[:, piece(owner)], coef.at[:, piece(owner)], coef_sem.at[owner])
+
+    def load(owner):
+        coef_load(owner).start()
+        block_load(owner).start()
+
+    each(count, load)
 
     barrier = pltpu.get_barrier_semaphore()
 
@@ -113,8 +119,12 @@
     def scatter(source, target, ssem, rsem):
         def push(step):
             owner = peer(step + 1)
-            remote(source.at[owner], target.at[me], ssem, rsem.at[me], owner).start()
+            remote(source.at[owner], target.at[me], ssem, rsem, owner).start()
         each(count - 1, push)
+
+    def all_in(target, rsem):
+        most = target.at[pl.ds(0, count - 1)]
+        remote(most, most, rsem, rsem, me + side).wait_recv()
 
     def arrive(target, rsem, owner):
         remote(target.at[owner], target.at[owner], rsem.at[owner], rsem.at[owner], owner).wait_recv()
@@ -129,7 +139,8 @@
             device_id={"var": 1 - var}, device_id_type=MESH,
         )
 
-    ids_row = facts[0:1, :]
+    code = codes[...].reshape(1, rows)
+    ids_row = (code // CODES).astype(F32)
     down_ranks = lax.broadcasted_iota(jnp.int32, (rows, rows), 0)
     along_ranks = lax.broadcasted_iota(jnp.int32, (rows, rows), 1)
     ids = jnp.sum(jnp.where(down_ranks == along_ranks, ids_row, 0.0), axis=1, keepdims=True)
@@ -151,12 +162,13 @@
         spot[owner] = jnp.max(jnp.where(match, ranks, -1), axis=0, keepdims=True)
 
     line = lax.broadcasted_iota(jnp.int32, (8, rows), 0)
-    labels = jnp.where(line == 0, facts[1:2, :], jnp.where(line == 1, facts[2:3, :], 0.0))
-    same = lax.broadcasted_iota(jnp.int32, (columns, columns), 0) == lax.broadcasted_iota(
-        jnp.int32, (columns, columns), 1
-    )
-    step_size = jnp.sum(jnp.where(same, facts[3:4, :columns], 0.0), axis=1, keepdims=True)
-    least = step_size * jnp.sum(jnp.where(same, facts[4:5, :columns], 0.0), axis=1, keepdims=True)
+    labels = jnp.where(line == 0, code % CODES // 2, jnp.where(line == 1, code % 2, 0)).astype(F32)
+    column = lax.broadcasted_iota(jnp.int32, (columns, 1), 0)
+    step_size = jnp.zeros((columns, 1), F32)
+    least = jnp.zeros((columns, 1), F32)
+    for number in range(columns):
+        step_size = jnp.where(column == number, rates[number], step_size)
+        least = jnp.where(column == number, rates[number] * rates[columns + number], least)
     column_fold = lax.rem(lax.broadcasted_iota(jnp.int32, (columns, rows), 0), FOLDS).astype(F32)
     trained = jnp.where(labels[0:1, :] != column_fold, 1.0, 0.0)
     counted = trained * labels[1:2, :]
@@ -171,24 +183,27 @@
     pl.semaphore_wait(barrier, count)
     scatter(place_out, place_in, p_ss, p_rs)
 
-    coef_load.wait()
-    for group in range(2):
-        low[group] = coef[group * few:(group + 1) * few, :].astype(BF16)
-        shard[group] = coef[group * few:(group + 1) * few, piece(me)]
-
-    def arrange():
+    def time_block():
         block = jnp.zeros((rows, width), jnp.int32)
-        each(count - 1, lambda step: arrive(place_in, p_rs, peer(step + 1)))
-        scattered(place_out, p_ss)
         for owner in range(1, count):
             block += jnp.where(place_in[owner] == ranks, owner, 0)
-        block = jnp.broadcast_to(jnp.sum(block, axis=1, keepdims=True), (rows, width))
-        in_totals = (lane - share) == block
+        return jnp.broadcast_to(jnp.sum(block, axis=1, keepdims=True), (rows, width))
+
+    def return_map():
+        block = time_block()
+        for owner in range(count):
+            span = slice(owner * width, (owner + 1) * width)
+            hit = place_in[owner] == ranks
+            to_id[:, span] = jnp.where(hit | ((lane == share) & (block > owner)), 1.0, 0.0).astype(BF16)
+
+    def arrange():
+        all_in(place_in, p_rs)
+        scattered(place_out, p_ss)
+        in_totals = (lane - share) == time_block()
         for owner in range(count):
             span = slice(owner * width, (owner + 1) * width)
             hit = place_in[owner] == ranks
             to_time[:, span] = jnp.where(hit | in_totals, 1.0, 0.0).astype(BF16)
-            to_id[:, span] = jnp.where(hit | ((lane == share) & (block > owner)), 1.0, 0.0).astype(BF16)
         spread = jnp.dot(labels.astype(BF16), to_time[...], preferred_element_type=F32)
         for owner in range(count):
             code_out[owner] = spread[:, owner * width:(owner + 1) * width]
@@ -206,7 +221,7 @@
             earlier[:, span] = jnp.where(back >= ranks, 1.0, 0.0).astype(BF16)
 
     def time_labels():
-        each(count - 1, lambda step: arrive(code_in, l_rs, peer(step + 1)))
+        all_in(code_in, l_rs)
         scattered(code_out, l_ss)
         labels_time = jnp.zeros((labels.shape[0], rows), F32)
         for owner in range(count):
@@ -221,12 +236,12 @@
         block = held_in.at[group, :, piece(me)]
         owner = me + side if hop is None else down(hop)
         index = (0 if hop is None else hop, band)
-        return remote(block, block, c_ss.at[index], c_rs.at[index], owner)
+        return remote(block, block, c_ss, c_rs.at[index], owner)
 
     def relay(held_in, end, hop, band, group):
         span = piece(up(hop))
         return remote(
-            held_in.at[group, :, span], end.at[group, :, span], fwd_ss.at[hop, band], fwd_rs.at[hop, band], me + side
+            held_in.at[group, :, span], end.at[group, :, span], fwd_ss, fwd_rs.at[hop, band], me + side
         )
 
     def tell_all(held_in, band, group):
@@ -239,12 +254,43 @@
             relay(held_in, end, hop, band, group).start()
         hops(go)
 
-    def told(held_in, end, band, group):
-        def go(hop):
-            tell(held_in, hop, band, group).wait_send()
-            relay(held_in, end, hop, band, group).wait_send()
-        hops(go)
-        tell(held_in, None, band, group).wait_send()
+    def told():
+        sent = low.at[:, :, pl.ds(0, half * part)]
+        remote(sent, sent, c_ss, c_ss, me + side).wait_send()
+        sent = low.at[:, :, pl.ds(0, (half - 1) * part)]
+        remote(sent, sent, fwd_ss, fwd_ss, me + side).wait_send()
+
+    upper = jnp.where(2 * me >= count, 1, 0)
+
+    def far(step):
+        return lax.rem(me + jnp.where(upper == 1, step + 1, count - 1 - step), count)
+
+    def spread_far(value, matrix, source, target, ssem, rsem):
+        split = halves(value)
+        near = upper * half
+
+        def block(first):
+            span = pl.ds(pl.multiple_of(first * width, width), half * width)
+            both = jnp.dot(split, matrix[:, span], preferred_element_type=F32)
+            block = both[:few] + both[few:]
+            for owner in range(half):
+                source[first + owner] = block[:, owner * width:(owner + 1) * width]
+
+        def push(owner):
+            remote(source.at[owner], target.at[me], ssem, rsem.at[me], owner).start()
+
+        block(half - near)
+        each(half, lambda step: push(lax.rem(half - near + lax.rem(me + step, half), count)))
+        block(near)
+        each(half - 1, lambda step: push(near + lax.rem(me + step + 1, half)))
+
+    def gather_far(source, target, rsem, matrix):
+        total = across2(source[me], matrix[:, slots(me)])
+        for step in range(count - 1):
+            owner = far(count - 2 - step)
+            arrive(target, rsem, owner)
+            total += across2(target[owner], matrix[:, slots(owner)])
+        return total
 
     def send_y(hop, band):
         return remote(out_y.at[hop, band], in_y.at[hop, band], y_ss, y_rs.at[hop, band], me + side)
@@ -254,6 +300,10 @@
 
     def add_part(owner, group):
         pred[group] += across(low[group, :, piece(owner)], geno[:, piece(owner)])
+
+    def both_parts(owner):
+        both = across(low[:, :, piece(owner)].reshape(columns, part), geno[:, piece(owner)])
+        return both.reshape(2, few, rows)
 
     def one_step(turn, first):
         own = lax.rem(var + turn, 2)
@@ -264,63 +314,51 @@
             pred[...] = jnp.zeros_like(pred)
 
             def add_block(owner):
+                coef_load(owner).wait()
+                for group in range(2):
+                    low[group, :, piece(owner)] = coef[group * few:(group + 1) * few, piece(owner)].astype(BF16)
                 block_load(owner).wait()
-                both = across(low[:, :, piece(owner)].reshape(columns, part), geno[:, piece(owner)])
-                pred[...] += both.reshape(2, few, rows)
+                pred[...] += both_parts(owner)
             each(count, add_block)
             swap.start()
+            for group in range(2):
+                shard[group] = coef[group * few:(group + 1) * few, piece(me)]
             arrange()
         else:
-            def begin(band, group):
-                pred[group] = across(low[group, :, piece(me)], geno[:, piece(me)])
-                tell(low, None, band, group).wait_recv()
-                add_part(me + side, group)
-
             def add_side(band, group):
                 def go(hop):
                     relay(low, low, hop, band, group).wait_recv()
                     add_part(up(hop) + side, group)
                 hops(go)
 
-            begin(0, other)
+            pred[...] = both_parts(me)
             pass_on(low, low, 0, other)
-            begin(1, own)
+            tell(low, None, 0, other).wait_recv()
+            tell(low, None, 1, own).wait_recv()
+            pred[...] += both_parts(me + side)
             hops(lambda hop: add_part(up(hop), other))
             pass_on(low, low, 1, own)
             add_side(0, other)
             swap.start()
             hops(lambda hop: add_part(up(hop), own))
             add_side(1, own)
-            told(low, low, 0, other)
-            told(low, low, 1, own)
+            told()
         swap.wait()
 
         weight = mask[own] * jnp.exp((pred[own] + half_recv[slot]) * scale_vars)
         held[...] = weight
-        spread = dot2(weight, to_time[...])
-        for owner in range(count):
-            out_a[owner] = spread[:, owner * width:(owner + 1) * width]
-        scatter(out_a, in_a, a_ss, a_rs)
+        spread_far(weight, to_time, out_a, in_a, a_ss, a_rs)
         if first:
             sums()
             time_labels()
-        risk = across2(out_a[me], later[:, slots(me)])
-        for step in range(count - 1):
-            owner = peer(step + 1)
-            arrive(in_a, a_rs, owner)
-            risk += across2(in_a[owner], later[:, slots(owner)])
+        total = gather_far(out_a, in_a, a_rs, later)
         events = kept_time[own]
-        ratio = events / jnp.where(events > 0, risk, 1.0)
-        spread = dot2(ratio, earlier[...])
-        for owner in range(count):
-            out_b[owner] = spread[:, owner * width:(owner + 1) * width]
-        scatter(out_b, in_b, b_ss, b_rs)
-        hazard = across2(out_b[me], to_id[:, slots(me)])
-        for step in range(count - 1):
-            owner = peer(step + 1)
-            arrive(in_b, b_rs, owner)
-            hazard += across2(in_b[owner], to_id[:, slots(owner)])
-        score[own] = (held[...] * hazard - kept[own]).astype(BF16)
+        ratio = events / jnp.where(events > 0, total, 1.0)
+        spread_far(ratio, earlier, out_b, in_b, b_ss, b_rs)
+        if first:
+            return_map()
+        total = gather_far(out_b, in_b, b_rs, to_id)
+        score[own] = (held[...] * total - kept[own]).astype(BF16)
         trade = swap_with(score.at[own], score.at[own], s_ss, s_rs)
         trade.start()
 
@@ -332,16 +370,11 @@
                 out_y[hop, band] = product(score[group], down(hop) + side).astype(BF16)
                 send_y(hop, band).start()
             hops(go)
-            go(0)
-
-        def keep(hop):
-            own_g[hop] = product(score[...].reshape(columns, rows), down(hop)).reshape(2, few, part)
-
-        give(0, own)
-        trade.wait()
-        give(1, other)
-        hops(keep)
-        keep(0)
+
+        def keep(group):
+            def go(hop):
+                own_g[hop, group] = product(score[group], down(hop))
+            hops(go)
 
         def pairs(band, group):
             def go(hop):
@@ -350,10 +383,22 @@
                 send_z(hop, band).start()
             hops(go)
 
+        give(0, own)
+        keep(own)
+        trade.wait()
+        give(1, other)
+        pairs(0, own)
+        out_y[0] = product(score[...].reshape(columns, rows), me + side).reshape(2, few, part).astype(BF16)
+        send_y(0, own).start()
+        send_y(0, other).start()
+        keep(other)
+        pairs(1, other)
+        own_g[0] = product(score[...].reshape(columns, rows), me).reshape(2, few, part)
+
         def update(band, group):
             total = own_g.at[0, group]
-            send_y(0, band).wait_recv()
-            total[...] += in_y[0, band].astype(F32)
+            send_y(0, group).wait_recv()
+            total[...] += in_y[0, group].astype(F32)
 
             def go(hop):
                 send_z(hop, band).wait_recv()
@@ -378,8 +423,6 @@
                 pl.when(turn < ITERS - 1)(spread_low)
                 pl.when(turn == ITERS - 1)(spread_change)
 
-        pairs(0, own)
-        pairs(1, other)
         update(0, own)
         update(1, other)
         scattered(out_a, a_ss)
@@ -391,16 +434,12 @@
     one_step(0, True)
     lax.fori_loop(1, ITERS, lambda turn, carry: (one_step(turn, False), carry)[1], 0)
 
-    def change_keep(hop):
-        span = piece(up(hop))
-        return pltpu.make_async_copy(change.at[:, :, span], change_out.at[:, :, span], keep_sem.at[hop])
-
-    def side_keep():
-        span = piece(me + side)
-        return pltpu.make_async_copy(change.at[:, :, span], change_out.at[:, :, span], end_sem.at[2])
+    def keep_change(owner):
+        span = piece(owner)
+        pltpu.make_async_copy(change.at[:, :, span], change_out.at[:, :, span], end_sem.at[2]).start()
 
     own = lax.rem(var + ITERS - 1, 2)
-    change_keep(0).start()
+    keep_change(me)
     low_keep = pltpu.make_async_copy(low, low_out, end_sem.at[0])
     low_keep.start()
     score_wide[...] = score[...].astype(F32)
@@ -408,17 +447,15 @@
     score_keep.start()
     pass_on(change, change_out, 0, own)
     pass_on(change, change_out, 1, 1 - own)
-    hops(lambda hop: change_keep(hop).start())
+    hops(lambda hop: keep_change(up(hop)))
     tell(change, None, 0, own).wait_recv()
     tell(change, None, 1, 1 - own).wait_recv()
-    side_keep().start()
-    told(change, change_out, 0, own)
-    told(change, change_out, 1, 1 - own)
+    keep_change(me + side)
+    told()
     low_keep.wait()
     score_keep.wait()
-    change_keep(0).wait()
-    hops(lambda hop: change_keep(hop).wait())
-    side_keep().wait()
+    kept_change = pl.ds(0, (half + 1) * part)
+    pltpu.make_async_copy(change.at[:, :, kept_change], change_out.at[:, :, kept_change], end_sem.at[2]).wait()
     hops(lambda hop: relay(change, change_out, hop, 0, own).wait_recv())
     hops(lambda hop: relay(change, change_out, hop, 1, 1 - own).wait_recv())
 
@@ -434,14 +471,10 @@
     part = variants // count
     few = columns // 2
 
-    def padded(value):
-        return jnp.pad(value, (0, rows - columns))
-
-    facts = jnp.stack([
-        time_order.astype(F32), fold_label.astype(F32), event_flag.astype(F32), padded(step_size), padded(penalty),
-    ])
+    codes = time_order * CODES + fold_label * 2 + event_flag
     vmem = pl.BlockSpec(memory_space=pltpu.VMEM)
     away = pl.BlockSpec(memory_space=pl.ANY)
+    hbm = pl.BlockSpec(memory_space=pltpu.HBM)
     dma = pltpu.SemaphoreType.DMA
     low, change, score = pl.pallas_call(
         functools.partial(path_kernel, count, 1.0 / math.sqrt(VARS), 1.0 / math.sqrt(rows * count)),
@@ -450,7 +483,7 @@
             jax.ShapeDtypeStruct((2, few, variants), BF16),
             jax.ShapeDtypeStruct((2, few, rows), F32),
         ),
-        in_specs=[away] * 2 + [vmem],
+        in_specs=[hbm] * 2 + [vmem] + [pl.BlockSpec(memory_space=pltpu.SMEM)],
         out_specs=(away, away, away),
         scratch_shapes=[
             pltpu.VMEM((rows, variants), BF16),
@@ -486,13 +519,13 @@
             pltpu.VMEM((few, rows), F32),
             pltpu.VMEM((2, few, rows), BF16),
             pltpu.VMEM((2, few, rows), F32),
-            dma((count,)), dma, dma((3,)), dma((half,)),
+            dma((count,)), dma((count,)), dma((3,)),
             dma, dma, dma, dma((2,)),
-        ] + [dma] * 6 + [dma((count,))] * 4 + [dma((half, 2))] * 6,
+        ] + [dma] * 10 + [dma((count,))] * 2 + [dma((half, 2))] * 4,
         compiler_params=pltpu.CompilerParams(
-            collective_id=0, has_side_effects=True, vmem_limit_bytes=60 * 1024 * 1024
+            collective_id=0, has_side_effects=True, vmem_limit_bytes=52 * 1024 * 1024
         ),
-    )(genotypes, coefficients, facts)
+    )(genotypes, coefficients, codes, jnp.concatenate([step_size, penalty]))
     coefs = low.astype(F32) + change.astype(F32)
     return coefs.reshape(columns, variants), score.astype(BF16).reshape(columns, rows)
 

time: 119 us -> 108 us (0.908)
  Pallas kernels: 110 us -> 104 us
  other arithmetic: 5.85 us -> 3.17 us
  local copies, waits for them, and re-layouts: 1.97 us -> 0 us
    pallas_call x1, Pallas kernels: 110 us -> 104 us  [local(): pl.pallas_call(functools.partial(path_kernel, count, 1.0 / math.sqrt(VARS...]
    convert_element_type x3 -> x0, other arithmetic: 2.07 us -> none  [the longest x1 0.69 us: local(): time_order.astype(F32)]
    pad x2 -> x0, local copies, waits for them, and re-layouts: 1.32 us -> none  [padded(): return jnp.pad(value, (0, rows - columns))]
    add x1, other arithmetic: 2.27 us -> 1.07 us  [local(): coefs = low.astype(F32) + change.astype(F32)]
where the time goes in v3:
time: 108 us
  Pallas kernels  104 us (96%)
  other arithmetic  3.17 us (3%)
    pallas_call x1, Pallas kernels, local(): pl.pallas_call(functools.partial(path_kernel, count, 1.0 / math.sqrt(VARS...  104 us

profile of v3, /device:TPU:0, one launch (start us, length us, event | category | flops | bytes accessed | tf_op | source)
XLA Modules:
  0.0 107.7 jit_solution(5638553355728864112)
XLA Ops:
  0.6 0.7 pad_maximum_fusion.rates
  1.4 0.7 add_add_fusion.codes
  2.1 103.9 %shard_map.86 = (bf16[2,16,8192]{2,1,0:T(8,128)(2,1)S(1)}, bf16[2,16,8192]{2,1,0:T(8,128)(2,1)S(1)}, f32[2,16,576]{2,1,0:T(8,128)S(1)}) custom-call(bf16[576,8192]{1,0:T(8,128)(2,1)} %geno_in.1, f32[32,8192]{1,0:T(8,128)} %coef_in.1, s32[576]{0:T(1024)S(1)} %add_add_fusion.codes, f32[64]{0:T(128)S(1)} %pad_maximum_fusion.rates), custom_call_target="tpu_custom_call" | custom-call | tf_op jit(solution)/shard_map/pallas_call | solution.py:479
  106.0 1.1 convert_add_fusion
  107.1 0.6 convert_element_type.11

commit v4 on v3

--- a/solution.py
+++ b/solution.py
@@ -49,7 +49,7 @@
 
 def path_kernel(
     count, scale_vars, scale_samples,
-    geno_in, coef_in, codes, rates,
+    geno_in, coef_in, facts,
     low_out, change_out, score_out,
     geno, coef, to_time, later, earlier, to_id, mask, kept, kept_time, place_out, place_in, spot, code_out, code_in,
     low, change, shard, pace, threshold, half_recv, out_a, in_a, out_b, in_b,
@@ -139,7 +139,8 @@
             device_id={"var": 1 - var}, device_id_type=MESH,
         )
 
-    code = codes[...].reshape(1, rows)
+    fact = facts[...].reshape(1, rows + 2 * columns)
+    code = fact[:, :rows].astype(jnp.int32)
     ids_row = (code // CODES).astype(F32)
     down_ranks = lax.broadcasted_iota(jnp.int32, (rows, rows), 0)
     along_ranks = lax.broadcasted_iota(jnp.int32, (rows, rows), 1)
@@ -163,12 +164,11 @@
 
     line = lax.broadcasted_iota(jnp.int32, (8, rows), 0)
     labels = jnp.where(line == 0, code % CODES // 2, jnp.where(line == 1, code % 2, 0)).astype(F32)
-    column = lax.broadcasted_iota(jnp.int32, (columns, 1), 0)
-    step_size = jnp.zeros((columns, 1), F32)
-    least = jnp.zeros((columns, 1), F32)
-    for number in range(columns):
-        step_size = jnp.where(column == number, rates[number], step_size)
-        least = jnp.where(column == number, rates[number] * rates[columns + number], least)
+    column = lax.broadcasted_iota(jnp.int32, (columns, 2 * columns), 0)
+    number = lax.broadcasted_iota(jnp.int32, (columns, 2 * columns), 1)
+    rates = fact[:, rows:]
+    step_size = jnp.sum(jnp.where(number == column, rates, 0.0), axis=1, keepdims=True)
+    least = step_size * jnp.sum(jnp.where(number == column + columns, rates, 0.0), axis=1, keepdims=True)
     column_fold = lax.rem(lax.broadcasted_iota(jnp.int32, (columns, rows), 0), FOLDS).astype(F32)
     trained = jnp.where(labels[0:1, :] != column_fold, 1.0, 0.0)
     counted = trained * labels[1:2, :]
@@ -336,11 +336,13 @@
             tell(low, None, 0, other).wait_recv()
             tell(low, None, 1, own).wait_recv()
             pred[...] += both_parts(me + side)
-            hops(lambda hop: add_part(up(hop), other))
             pass_on(low, low, 1, own)
+
+            def add_up(hop):
+                pred[...] += both_parts(up(hop))
+            hops(add_up)
             add_side(0, other)
             swap.start()
-            hops(lambda hop: add_part(up(hop), own))
             add_side(1, own)
             told()
         swap.wait()
@@ -472,6 +474,7 @@
     few = columns // 2
 
     codes = time_order * CODES + fold_label * 2 + event_flag
+    facts = jnp.concatenate([codes.astype(F32), step_size, penalty])
     vmem = pl.BlockSpec(memory_space=pltpu.VMEM)
     away = pl.BlockSpec(memory_space=pl.ANY)
     hbm = pl.BlockSpec(memory_space=pltpu.HBM)
@@ -483,7 +486,7 @@
             jax.ShapeDtypeStruct((2, few, variants), BF16),
             jax.ShapeDtypeStruct((2, few, rows), F32),
         ),
-        in_specs=[hbm] * 2 + [vmem] + [pl.BlockSpec(memory_space=pltpu.SMEM)],
+        in_specs=[hbm] * 2 + [vmem],
         out_specs=(away, away, away),
         scratch_shapes=[
             pltpu.VMEM((rows, variants), BF16),
@@ -525,7 +528,7 @@
         compiler_params=pltpu.CompilerParams(
             collective_id=0, has_side_effects=True, vmem_limit_bytes=52 * 1024 * 1024
         ),
-    )(genotypes, coefficients, codes, jnp.concatenate([step_size, penalty]))
+    )(genotypes, coefficients, facts)
     coefs = low.astype(F32) + change.astype(F32)
     return coefs.reshape(columns, variants), score.astype(BF16).reshape(columns, rows)
 

time: 108 us -> 105 us (0.972)
  Pallas kernels: 104 us -> 101 us
    pallas_call x1, Pallas kernels: 104 us -> 101 us  [local(): pl.pallas_call(functools.partial(path_kernel, count, 1.0 / math.sqrt(VARS...]
where the time goes in v4:
time: 105 us
  Pallas kernels  101 us (96%)
  other arithmetic  3.17 us (3%)
    pallas_call x1, Pallas kernels, local(): pl.pallas_call(functools.partial(path_kernel, count, 1.0 / math.sqrt(VARS...  101 us

profile of v4, /device:TPU:0, one launch (start us, length us, event | category | flops | bytes accessed | tf_op | source)
XLA Modules:
  0.0 104.8 jit_solution(328576340873980668)
XLA Ops:
  0.6 0.7 add_convert_fusion
  1.4 0.7 pad_maximum_fusion.facts
  2.1 101.0 %shard_map.86 = (bf16[2,16,8192]{2,1,0:T(8,128)(2,1)S(1)}, bf16[2,16,8192]{2,1,0:T(8,128)(2,1)S(1)}, f32[2,16,576]{2,1,0:T(8,128)S(1)}) custom-call(bf16[576,8192]{1,0:T(8,128)(2,1)} %geno_in.1, f32[32,8192]{1,0:T(8,128)} %coef_in.1, f32[640]{0:T(1024)S(1)} %pad_maximum_fusion.facts), custom_call_target="tpu_custom_call" | custom-call | tf_op jit(solution)/shard_map/pallas_call | solution.py:482
  103.1 1.1 %convert_add_fusion = f32[2,16,8192]{2,1,0:T(8,128)} fusion(bf16[2,16,8192]{2,1,0:T(8,128)(2,1)S(1)} %get-tuple-element.6, bf16[2,16,8192]{2,1,0:T(8,128)(2,1)S(1)} %get-tuple-element.5), kind=kLoop, calls=%fused_computation | loop fusion | flops 786432 | bytes 2097152 | tf_op jit(solution)/shard_map/add | solution.py:532
  104.2 0.6 convert_element_type.15

commit v5 on v4

--- a/solution.py
+++ b/solution.py
@@ -80,9 +80,9 @@
     def piece(owner):
         return pl.ds(pl.multiple_of(owner * part, part), part)
 
-    def hops(body):
+    def hops(body, order=(2, 1, 3)):
         if half <= 8:
-            for hop in sorted(range(1, half), key=lambda hop: (abs(2 * hop - half), hop)):
+            for hop in (order if half == 4 else range(1, half)):
                 body(hop)
         else:
             lax.fori_loop(1, half, lambda hop, carry: (body(hop), carry)[1], 0)
@@ -145,11 +145,8 @@
     down_ranks = lax.broadcasted_iota(jnp.int32, (rows, rows), 0)
     along_ranks = lax.broadcasted_iota(jnp.int32, (rows, rows), 1)
     ids = jnp.sum(jnp.where(down_ranks == along_ranks, ids_row, 0.0), axis=1, keepdims=True)
-    owner_row = jnp.zeros_like(ids_row)
-    owner_of = jnp.zeros_like(ids)
-    for owner in range(1, count):
-        owner_row += jnp.where(ids_row >= owner * rows, 1.0, 0.0)
-        owner_of += jnp.where(ids >= owner * rows, 1.0, 0.0)
+    owner_row = jnp.floor((ids_row + 0.5) * (1.0 / rows))
+    owner_of = jnp.floor((ids + 0.5) * (1.0 / rows))
     before = jnp.sum(
         jnp.where((owner_row == owner_of) & (along_ranks < down_ranks), 1.0, 0.0), axis=1, keepdims=True
     )
@@ -371,7 +368,7 @@
             def go(hop):
                 out_y[hop, band] = product(score[group], down(hop) + side).astype(BF16)
                 send_y(hop, band).start()
-            hops(go)
+            hops(go, (2, 1, 3) if band == 0 else (1, 3, 2))
 
         def keep(group):
             def go(hop):
@@ -383,7 +380,7 @@
                 send_y(hop, band).wait_recv()
                 out_z[hop, band] = (own_g[hop, group] + in_y[hop, band].astype(F32)).astype(BF16)
                 send_z(hop, band).start()
-            hops(go)
+            hops(go, (2, 1, 3) if band == 0 else (1, 3, 2))
 
         give(0, own)
         keep(own)

time: 105 us -> 104 us (level)
  no operation moved by 1% of the time
where the time goes in v5:
time: 104 us
  Pallas kernels  100 us (96%)
  other arithmetic  3.17 us (3%)
    pallas_call x1, Pallas kernels, local(): pl.pallas_call(functools.partial(path_kernel, count, 1.0 / math.sqrt(VARS...  100 us

profile of v5, /device:TPU:0, one launch (start us, length us, event | category | flops | bytes accessed | tf_op | source)
XLA Modules:
  0.0 104.3 jit_solution(17687951160740827218)
XLA Ops:
  0.6 0.7 add_convert_fusion
  1.4 0.7 pad_maximum_fusion.facts
  2.1 100.4 %shard_map.86 = (bf16[2,16,8192]{2,1,0:T(8,128)(2,1)S(1)}, bf16[2,16,8192]{2,1,0:T(8,128)(2,1)S(1)}, f32[2,16,576]{2,1,0:T(8,128)S(1)}) custom-call(bf16[576,8192]{1,0:T(8,128)(2,1)} %geno_in.1, f32[32,8192]{1,0:T(8,128)} %coef_in.1, f32[640]{0:T(1024)S(1)} %pad_maximum_fusion.facts), custom_call_target="tpu_custom_call" | custom-call | tf_op jit(solution)/shard_map/pallas_call | solution.py:479
  102.6 1.1 %convert_add_fusion = f32[2,16,8192]{2,1,0:T(8,128)} fusion(bf16[2,16,8192]{2,1,0:T(8,128)(2,1)S(1)} %get-tuple-element.6, bf16[2,16,8192]{2,1,0:T(8,128)(2,1)S(1)} %get-tuple-element.5), kind=kLoop, calls=%fused_computation | loop fusion | flops 786432 | bytes 2097152 | tf_op jit(solution)/shard_map/add | solution.py:529
  103.6 0.6 convert_element_type.15

commit v6 on v5

--- a/solution.py
+++ b/solution.py
@@ -387,10 +387,10 @@
         trade.wait()
         give(1, other)
         pairs(0, own)
+        keep(other)
         out_y[0] = product(score[...].reshape(columns, rows), me + side).reshape(2, few, part).astype(BF16)
         send_y(0, own).start()
         send_y(0, other).start()
-        keep(other)
         pairs(1, other)
         own_g[0] = product(score[...].reshape(columns, rows), me).reshape(2, few, part)
 

time: 104 us -> 104 us (level)
  no operation moved by 1% of the time
where the time goes in v6:
time: 104 us
  Pallas kernels  100 us (96%)
  other arithmetic  3.17 us (3%)
    pallas_call x1, Pallas kernels, local(): pl.pallas_call(functools.partial(path_kernel, count, 1.0 / math.sqrt(VARS...  100 us

profile of v6, /device:TPU:0, one launch (start us, length us, event | category | flops | bytes accessed | tf_op | source)
XLA Modules:
  0.0 104.0 jit_solution(6188092537083129092)
XLA Ops:
  0.6 0.7 add_convert_fusion
  1.4 0.7 pad_maximum_fusion.facts
  2.1 100.2 %shard_map.86 = (bf16[2,16,8192]{2,1,0:T(8,128)(2,1)S(1)}, bf16[2,16,8192]{2,1,0:T(8,128)(2,1)S(1)}, f32[2,16,576]{2,1,0:T(8,128)S(1)}) custom-call(bf16[576,8192]{1,0:T(8,128)(2,1)} %geno_in.1, f32[32,8192]{1,0:T(8,128)} %coef_in.1, f32[640]{0:T(1024)S(1)} %pad_maximum_fusion.facts), custom_call_target="tpu_custom_call" | custom-call | tf_op jit(solution)/shard_map/pallas_call | solution.py:479
  102.3 1.1 %convert_add_fusion = f32[2,16,8192]{2,1,0:T(8,128)} fusion(bf16[2,16,8192]{2,1,0:T(8,128)(2,1)S(1)} %get-tuple-element.6, bf16[2,16,8192]{2,1,0:T(8,128)(2,1)S(1)} %get-tuple-element.5), kind=kLoop, calls=%fused_computation | loop fusion | flops 786432 | bytes 2097152 | tf_op jit(solution)/shard_map/add | solution.py:529
  103.4 0.6 convert_element_type.15
